TPU v7x, 1024 devices: a whole 8x8x8 slice. The times are simulated.
1024 devices in a mesh: dp: 8 (over x), pipe: 16 (over z, core), tensor: 8 (over y).
Axes of the slice: x: 8, y: 8, z: 8, core: 2. Of those that a mesh axis runs over, the one named last changes fastest.
Arguments:
- hidden: bfloat16 [1024, 8192], P(('dp', 'pipe'), 'tensor'), parts along dimension 0, may hold values from -15 to 15
- gain: float32 [8192], replicated, may hold values from 0.1 to 1.9
- lm_head: bfloat16 [79872, 8192], P(('pipe', 'tensor')), may hold values from -0.29831067 to 0.29831067
- targets: int32 [1024], P('dp'), parts along dimension 0, may hold values from 0 to 79871
- banned: int32 [79872], P(('pipe', 'tensor')), may hold values 0 or 1
Outputs:
- loss: float32 [1024], P(('dp', 'pipe')), parts along dimension 0
- grad_hidden: bfloat16 [1024, 8192], P(('dp', 'pipe'), 'tensor'), parts along dimension 0
There are 8 independent parts, one for each index of `dp`. A program takes and returns all parts, laid end to end along the dimension named above; an argument that names none is the same for every part. Nothing has to cross between parts.
All inputs are finite; a program needn't handle non-finite values. No bound on the sum of `banned` on one device may be relied on, other than what follows from the above.
Results may differ from a plain program's by a relative error of at most 0.0056.
Values may be sent and summed in bfloat16 or wider, within the bound.
No kernel may reach another device: no remote copies, remote signals or barrier semaphores. Data moves between devices by JAX's collectives and lax.ppermute only.
A program may use at most 64 MiB of HBM per device.

v0:
```python
import jax
import jax.numpy as jnp
from jax import lax
from jax.sharding import PartitionSpec as P

EPSILON = 1e-05


def local(hidden, gain, lm_head, targets, banned):
    pipe_count = lax.axis_size("pipe")
    tensor_count = lax.axis_size("tensor")
    pipe_index = lax.axis_index("pipe")
    tensor_index = lax.axis_index("tensor")
    own_tokens, own_width = hidden.shape
    full_width = lm_head.shape[1]
    vocab_rows = lm_head.shape[0]
    hidden_wide = hidden.astype(jnp.float32)
    gain_own = lax.dynamic_slice_in_dim(gain, tensor_index * own_width, own_width)
    squares = lax.psum(jnp.sum(hidden_wide * hidden_wide, axis=1), "tensor")
    inverse_own = lax.rsqrt(squares / full_width + EPSILON)
    normed_own = (hidden_wide * inverse_own[:, None] * gain_own[None, :]).astype(jnp.bfloat16)
    section_rows = lax.all_gather(normed_own, "tensor", axis=1, tiled=True)
    logits = jnp.einsum(
        "td,vd->tv",
        lax.all_gather(section_rows, "pipe", axis=0, tiled=True),
        lm_head,
        preferred_element_type=jnp.float32,
    )
    vocab_start = (pipe_index * tensor_count + tensor_index) * vocab_rows
    vocab_ids = vocab_start + jnp.arange(vocab_rows, dtype=jnp.int32)
    is_target = vocab_ids[None, :] == targets[:, None]
    allowed = (banned[None, :] == 0) | is_target
    local_max = jnp.max(jnp.where(allowed, logits, -1e30), axis=1)
    target_local = jnp.sum(jnp.where(is_target, logits, 0.0), axis=1)
    row_max = lax.pmax(local_max, ("pipe", "tensor"))
    shifted = jnp.where(allowed, jnp.exp(logits - row_max[:, None]), 0.0)
    sum_exp, target_logit = lax.psum((jnp.sum(shifted, axis=1), target_local), ("pipe", "tensor"))
    loss_all = row_max + jnp.log(sum_exp) - target_logit
    loss_own = lax.dynamic_slice_in_dim(loss_all, pipe_index * own_tokens, own_tokens)
    dlogits = (shifted / sum_exp[:, None] - is_target.astype(jnp.float32)).astype(jnp.bfloat16)
    head_split = lm_head.reshape(vocab_rows, tensor_count, own_width)
    logit_split = dlogits.reshape(pipe_count, own_tokens, vocab_rows)
    terms = jnp.einsum("ptv,vkd->pktd", logit_split, head_split, preferred_element_type=jnp.float32)
    terms = terms.reshape(pipe_count * tensor_count * own_tokens, own_width)
    grad_normed = lax.psum_scatter(terms, ("pipe", "tensor"), scatter_dimension=0, tiled=True)
    scaled = hidden_wide * inverse_own[:, None]
    gated = grad_normed * gain_own[None, :]
    inner = lax.psum(jnp.sum(gated * scaled, axis=1), "tensor") / full_width
    grad_hidden = (inverse_own[:, None] * (gated - scaled * inner[:, None])).astype(jnp.bfloat16)
    return (loss_own, grad_hidden)


def solution(mesh):
    in_specs = (
        P(("dp", "pipe"), "tensor"),
        P(),
        P(("pipe", "tensor"), None),
        P("dp"),
        P(("pipe", "tensor")),
    )
    out_specs = (P(("dp", "pipe")), P(("dp", "pipe"), "tensor"))
    return jax.shard_map(local, mesh=mesh, in_specs=in_specs, out_specs=out_specs, check_vma=False)
```

profile of v0, /device:TPU:14, one launch (start us, length us, event | category | flops | bytes accessed | tf_op | source)
XLA Modules:
  0.0 854.6 jit_solution(15273074947341388747)
XLA Ops:
  7.2 0.0 all-gather.2.cloned.1.call-start
  7.2 0.8 fusion.18
  8.1 18.4 %psum.28 = f32[8]{0:T(128)S(1)} all-reduce(f32[8]{0:T(128)S(1)} %fusion.18), channel_id=1, replica_groups=mesh['dp'=8,'pipe'=16,'tensor'=8] {'tensor'}, use_global_device_ids=true, to_apply=%region_1.0 | all-reduce | flops 8 | bytes 64 | tf_op jit(solution)/shard_map/psum | solution.py:19
  26.5 0.7 dynamic_slice.6
  27.2 0.8 fusion.13
  28.0 26.6 %all_gather.6 = bf16[8,8192]{1,0:T(8,128)(2,1)} all-gather(bf16[8,1024]{1,0:T(8,128)(2,1)S(1)} %fusion.13), channel_id=1, replica_groups=mesh['dp'=8,'pipe'=16,'tensor'=8] {'tensor'}, dimensions={1}, use_global_device_ids=true | all-gather | bytes 147456 | tf_op jit(solution)/shard_map/all_gather | solution.py:22
  54.5 0.0 all-gather.2.cloned.1.call-update
  54.5 0.0 reduce-scatter.2.cloned.1.call-start
  54.6 0.7 broadcast_compare_fusion
  55.3 54.0 %all-gather.2.cloned.1.call-done = bf16[128,8192]{1,0:T(8,128)(2,1)} async-done(((bf16[8,8192]{1,0:T(8,128)(2,1)}), bf16[128,8192]{1,0:T(8,128)(2,1)}) %all-gather.2.cloned.1.call-update) | async-done | bytes 2097168 | tf_op jit(solution)/shard_map/all_gather | solution.py:25
  109.3 6.3 fusion.4
  115.6 250.6 %pmax.7 = f32[128]{0:T(128)S(1)} all-reduce(f32[128]{0:T(128)S(1)} %get-tuple-element.6), channel_id=1, replica_groups=mesh['dp'=8,'pipe'=16,'tensor'=8] {'pipe','tensor'}, use_global_device_ids=true, to_apply=%region_3.4 | all-reduce | flops 128 | bytes 1024 | tf_op jit(solution)/shard_map/pmax | solution.py:35
  366.1 0.2 fusion.8
  366.4 246.8 %all-reduce = (f32[128]{0:T(128)S(1)}, f32[128]{0:T(128)S(1)}) all-reduce(f32[128]{0:T(128)S(1)} %get-tuple-element.3, f32[128]{0:T(128)S(1)} %get-tuple-element.2), channel_id=1, replica_groups=mesh['dp'=8,'pipe'=16,'tensor'=8] {'pipe','tensor'}, use_global_device_ids=true, to_apply=%region_7.8 | all-reduce | flops 256 | bytes 2048 | tf_op jit(solution)/shard_map/psum | solution.py:37
  613.2 0.2 fusion.7
  613.5 0.2 copy.9
  613.6 0.0 copy-start
  613.6 7.6 fusion
  621.3 0.0 reduce-scatter.2.cloned.1.call-update
  621.3 207.5 %reduce-scatter.2.cloned.1.call-done = f32[8,1024]{1,0:T(8,128)} async-done(((f32[1024,1024]{1,0:T(8,128)}), f32[8,1024]{1,0:T(8,128)}) %reduce-scatter.2.cloned.1.call-update) | async-done | bytes 32784 | tf_op jit(solution)/shard_map/reduce_scatter | solution.py:45
  828.8 0.9 fusion.14
  829.8 0.6 dynamic_slice.7
  830.4 15.9 %psum.31 = f32[8]{0:T(128)S(1)} all-reduce(f32[8]{0:T(128)S(1)} %fusion.14), channel_id=1, replica_groups=mesh['dp'=8,'pipe'=16,'tensor'=8] {'tensor'}, use_global_device_ids=true, to_apply=%region_10.11 | all-reduce | flops 8 | bytes 64 | tf_op jit(solution)/shard_map/psum | solution.py:48
  846.3 1.4 fusion.17
  (7 shorter events, 0.0 us)
Async XLA Ops:
  7.2 102.1 %all-gather.2.cloned.1.call-start = ((), (), s32[]{:S(2)}) async-start(), calls=%async_computation.1 | async-start | bytes 2228224 | tf_op jit(solution)/shard_map/all_gather | solution.py:25
  54.5 774.3 %reduce-scatter.2.cloned.1.call-start = ((), (), s32[]{:S(2)}) async-start(), calls=%async_computation.2 | async-start | bytes 4227072 | tf_op jit(solution)/shard_map/reduce_scatter | solution.py:45
  55.3 310.8 %copy-start.1 = (s32[128]{0:T(128)S(1)}, s32[128]{0:T(128)}, u32[]{:S(2)}) copy-start(s32[128]{0:T(128)} %param.8) | copy-start | bytes 1540
  613.6 215.2 %copy-start = (bf16[8,1024]{1,0:T(8,128)(2,1)S(1)}, bf16[8,1024]{1,0:T(8,128)(2,1)}, u32[]{:S(2)}) copy-start(bf16[8,1024]{1,0:T(8,128)(2,1)} %param.5) | copy-start | bytes 49156
Sparse Core Ops, SparseCore 0:
  54.7 54.5 all-gather.1
  621.4 207.3 reduce-scatter.1
where the time goes:
time: 855 us
  blocking collectives  558 us (65%)
  waiting for transfers between devices  262 us (31%)
  between operations  14.1 us (2%)
  matrix products  13.9 us (2%)
    pmax x1, blocking collectives, local(): row_max = lax.pmax(local_max, ('pipe', 'tensor'))  251 us
    psum x1, blocking collectives, local(): lax.psum((jnp.sum(shifted, axis=1), target_local), ('pipe', 'tensor'))  247 us
    reduce_scatter x1, waiting for transfers between devices, local(): lax.psum_scatter(terms, ('pipe', 'tensor'), scatter_dimension=0, tiled=True)  208 us
    all_gather x1, waiting for transfers between devices, local(): lax.all_gather(section_rows, 'pipe', axis=0, tiled=True)  54 us
    all_gather x1, blocking collectives, local(): section_rows = lax.all_gather(normed_own, 'tensor', axis=1, tiled=True)  26.6 us
    psum x1, blocking collectives, local(): squares = lax.psum(jnp.sum(hidden_wide * hidden_wide, axis=1), 'tensor')  18.4 us
  transfers between devices with their start and end apart: 2, of which 2 were waited for; matrix products, arithmetic and copies ran while one was open for 0% of the time, Pallas kernels for 0%

commit v1 on v0

v1 whole, which is shorter than its diff:
```python
import jax
import jax.numpy as jnp
from jax import lax
from jax.sharding import Mesh
from jax.sharding import PartitionSpec as P

EPSILON = 1e-05
LOWEST = -1e30
CORES = 2
PLANE = ("z", "tensor")


def swap_cores(values):
    return lax.ppermute(values, "core", [(0, 1), (1, 0)])


def local(hidden, gain, lm_head, targets, banned):
    z_count = lax.axis_size("z")
    tensor_count = lax.axis_size("tensor")
    chips = z_count * tensor_count
    z_index = lax.axis_index("z")
    core_index = lax.axis_index("core")
    tensor_index = lax.axis_index("tensor")
    own_tokens, own_width = hidden.shape
    vocab_rows, full_width = lm_head.shape
    tokens = targets.shape[0]

    sent = jnp.broadcast_to(hidden[None], (chips, own_tokens, own_width))
    got = lax.all_to_all(sent, PLANE, 0, 0, tiled=True)
    both = jnp.stack([got, swap_cores(got)])
    rows = both.reshape(CORES, z_count, tensor_count, own_tokens, own_width)
    rows = rows.transpose(0, 1, 3, 2, 4).reshape(tokens, full_width).astype(jnp.float32)
    inverse = lax.rsqrt(jnp.mean(rows * rows, axis=1) + EPSILON)
    normed = (rows * inverse[:, None] * gain[None, :]).astype(jnp.bfloat16)
    logits = jnp.einsum("td,vd->tv", normed, lm_head, preferred_element_type=jnp.float32)

    by_core = targets.reshape(z_count, CORES, own_tokens)
    row_targets = jnp.where(core_index == 0, by_core, by_core[:, ::-1]).transpose(1, 0, 2).reshape(tokens)
    vocab_start = ((z_index * CORES + core_index) * tensor_count + tensor_index) * vocab_rows
    vocab_ids = vocab_start + jnp.arange(vocab_rows, dtype=jnp.int32)
    is_target = vocab_ids[None, :] == row_targets[:, None]
    allowed = (banned[None, :] == 0) | is_target
    local_max = jnp.max(jnp.where(allowed, logits, LOWEST), axis=1)
    below = logits - local_max[:, None]
    shifted = jnp.where(allowed, jnp.exp(below), 0.0)
    local_sum = jnp.sum(shifted, axis=1)
    local_dot = jnp.sum(jnp.where(allowed, shifted * below, 0.0), axis=1)
    local_target = jnp.sum(jnp.where(is_target, logits, 0.0), axis=1)

    def combine(stats):
        maxima = stats[:, 0]
        top = jnp.max(maxima, axis=0)
        gap = maxima - top[None]
        weight = jnp.exp(gap)
        total = jnp.sum(weight * stats[:, 1], axis=0)
        dot = jnp.sum(weight * (stats[:, 2] + stats[:, 1] * gap), axis=0)
        return jnp.stack([top, total, dot, jnp.sum(stats[:, 3], axis=0)])

    mine = jnp.stack([local_max, local_sum, local_dot, local_target])
    halves = mine.reshape(4, CORES, tokens // CORES)
    theirs = swap_cores(halves[:, ::-1]).reshape(4, tokens)
    pair = combine(jnp.stack([mine, theirs]))
    everyone = lax.all_to_all(jnp.broadcast_to(pair[None], (chips,) + pair.shape), PLANE, 0, 0, tiled=True)

    share = jnp.exp(local_max - pair[0])
    weights = jnp.where(is_target, 0.0, shifted).astype(jnp.bfloat16)
    picks = is_target.astype(jnp.bfloat16)
    head_split = lm_head.reshape(vocab_rows, tensor_count, own_width)

    def split_terms(left, scale):
        terms = jnp.einsum("tv,vkd->tkd", left, head_split, preferred_element_type=jnp.float32)
        if scale is not None:
            terms = terms * scale[:, None, None]
        terms = terms.astype(jnp.bfloat16).reshape(CORES, z_count, own_tokens, tensor_count, own_width)
        return terms.transpose(0, 1, 3, 2, 4)

    terms = jnp.stack([split_terms(weights, share), split_terms(picks, None)], axis=1)
    terms = terms[0].astype(jnp.float32) + swap_cores(terms[1]).astype(jnp.float32)

    top, total, dot, target_logit = combine(everyone)
    loss = top + jnp.log(total) - target_logit
    scale = jnp.exp(pair[0] - top) / total
    target_scale = (jnp.exp(target_logit - top) / total - 1.0).astype(jnp.bfloat16).astype(jnp.float32)
    inner = (dot / total - (target_logit - top)) / full_width

    def by_piece(values):
        return values[: tokens // CORES].reshape(z_count, 1, own_tokens, 1)

    pieces = terms[0] * by_piece(scale) + terms[1] * by_piece(target_scale)
    pieces = pieces.astype(jnp.bfloat16).reshape(chips, own_tokens, own_width)
    grad_normed = jnp.sum(lax.all_to_all(pieces, PLANE, 0, 0, tiled=True).astype(jnp.float32), axis=0)

    def own_rows(values):
        return lax.dynamic_slice_in_dim(values, z_index * own_tokens, own_tokens)

    gain_own = lax.dynamic_slice_in_dim(gain, tensor_index * own_width, own_width)
    inverse_own = own_rows(inverse)[:, None]
    scaled = hidden.astype(jnp.float32) * inverse_own
    gated = grad_normed * gain_own[None, :]
    grad_hidden = (inverse_own * (gated - scaled * own_rows(inner)[:, None])).astype(jnp.bfloat16)
    return (own_rows(loss), grad_hidden)


def solution(mesh):
    dp, pipe, tensor = mesh.devices.shape
    fine = Mesh(mesh.devices.reshape(dp, pipe // CORES, CORES, tensor), ("dp", "z", "core", "tensor"))
    section = ("dp", "z", "core")
    in_specs = (
        P(section, "tensor"),
        P(),
        P(("z", "core", "tensor"), None),
        P("dp"),
        P(("z", "core", "tensor")),
    )
    out_specs = (P(section), P(section, "tensor"))
    return jax.shard_map(local, mesh=fine, in_specs=in_specs, out_specs=out_specs, check_vma=False)
```

time: 855 us -> 151 us (0.18)
  blocking collectives: 558 us -> 53 us
  waiting for transfers between devices: 262 us -> 42.4 us
  starting transfers between devices: 0.08 us -> 19.4 us
  between operations: 14.1 us -> 0.91 us
    psum x3 -> x0, blocking collectives: 281 us -> none  [the longest x1 247 us: local(): lax.psum((jnp.sum(shifted, axis=1), target_local), ('pipe', 'tensor'))]
    pmax x1 -> x0, blocking collectives: 251 us -> none  [local(): row_max = lax.pmax(local_max, ('pipe', 'tensor'))]
    reduce_scatter x1 -> x0, waiting for transfers between devices: 208 us -> none  [local(): lax.psum_scatter(terms, ('pipe', 'tensor'), scatter_dimension=0, tiled=True)]
    all_gather x1 -> x0, waiting for transfers between devices: 54 us -> none  [local(): lax.all_gather(section_rows, 'pipe', axis=0, tiled=True)]
    all_to_all x0 -> x1, blocking collectives: none -> 53 us  [local(): got = lax.all_to_all(sent, PLANE, 0, 0, tiled=True)]
    all_to_all x0 -> x2, waiting for transfers between devices: none -> 34.8 us  [the longest x1 29.1 us: local(): lax.all_to_all(pieces, PLANE, 0, 0, tiled=True).astype(jnp.float32)]
    all_gather x1 -> x0, blocking collectives: 26.6 us -> none  [local(): section_rows = lax.all_gather(normed_own, 'tensor', axis=1, tiled=True)]
    all_to_all x0 -> x2, starting transfers between devices: none -> 13.6 us  [the longest x1 7.17 us: local(): lax.all_to_all(pieces, PLANE, 0, 0, tiled=True).astype(jnp.float32)]
  transfers between devices with their start and end apart: 2 -> 5, of which waited for: 2 -> 5; matrix products, arithmetic and copies ran while one was open for 0% -> 6% of each run, Pallas kernels for 0% -> 0%
where the time goes in v1:
time: 151 us; the launch traced here: 150 us
  blocking collectives  53 us (35%)
  waiting for transfers between devices  42.4 us (28%)
  matrix products  20.4 us (14%)
  starting transfers between devices  19.4 us (13%)
  other arithmetic  9.74 us (6%)
  local copies, waits for them, and re-layouts  4.62 us (3%)
    all_to_all x1, blocking collectives, local(): got = lax.all_to_all(sent, PLANE, 0, 0, tiled=True)  53 us
    all_to_all x1, waiting for transfers between devices, local(): lax.all_to_all(pieces, PLANE, 0, 0, tiled=True).astype(jnp.float32)  29.1 us
    dot_general x2, matrix products, split_terms(): jnp.einsum('tv,vkd->tkd', left, head_split, preferred_element_type=jnp.fl...  13.3 us
    ppermute x3, waiting for transfers between devices, swap_cores(): return lax.ppermute(values, 'core', [(0, 1), (1, 0)])  7.59 us
    all_to_all x1, starting transfers between devices, local(): lax.all_to_all(pieces, PLANE, 0, 0, tiled=True).astype(jnp.float32)  7.17 us
    dot_general x1, matrix products, local(): jnp.einsum('td,vd->tv', normed, lm_head, preferred_element_type=jnp.float32)  7.02 us
    all_to_all x1, starting transfers between devices, local(): lax.all_to_all(jnp.broadcast_to(pair[None], (chips,) + pair.shape), PLANE...  6.41 us
    ppermute x3, starting transfers between devices, swap_cores(): return lax.ppermute(values, 'core', [(0, 1), (1, 0)])  5.86 us
  transfers between devices with their start and end apart: 5, of which 5 were waited for; matrix products, arithmetic and copies ran while one was open for 6% of the time, Pallas kernels for 0%

profile of v1, /device:TPU:14, one launch (start us, length us, event | category | flops | bytes accessed | tf_op | source)
XLA Modules:
  0.0 150.4 jit_solution(14082939563197851520)
XLA Ops:
  0.6 0.8 broadcast_in_dim.14
  1.5 53.0 %all_to_all.15 = bf16[64,8,1024]{2,1,0:T(8,128)(2,1)S(1)} all-to-all(bf16[64,8,1024]{2,1,0:T(8,128)(2,1)S(1)} %broadcast_in_dim.14), channel_id=1, replica_groups=mesh['dp'=8,'z'=8,'core'=2,'tensor'=8] {'z','tensor'}, dimensions={0} | all-to-all | bytes 2097152 | tf_op jit(solution)/shard_map/all_to_all | solution.py:29
  54.5 1.9 %collective-permute-start = (bf16[64,8,1024]{2,1,0:T(8,128)(2,1)S(1)}, bf16[64,8,1024]{2,1,0:T(8,128)(2,1)S(1)}, u32[]{:S(2)}, u32[]{:S(2)}) collective-permute-start(bf16[64,8,1024]{2,1,0:T(8,128)(2,1)S(1)} %all_to_all.15), channel_id=1, source_target_pairs={{0,8},{8,0},{1,9},{9,1},{2,10},{10,2},{3,11},{11,3},{4,12},{12,4},... | collective-permute-start | bytes 3145736 | tf_op jit(solution)/shard_map/ppermute | solution.py:14
  56.7 2.3 %collective-permute-done = bf16[64,8,1024]{2,1,0:T(8,128)(2,1)S(1)} collective-permute-done((bf16[64,8,1024]{2,1,0:T(8,128)(2,1)S(1)}, bf16[64,8,1024]{2,1,0:T(8,128)(2,1)S(1)}, u32[]{:S(2)}, u32[]{:S(2)}) %collective-permute-start) | collective-permute-done | bytes 1048608 | tf_op jit(solution)/shard_map/ppermute | solution.py:14
  59.0 0.5 multiply_reduce_fusion
  59.6 2.2 %maximum_convert_fusion = f32[2,8,8,8,1024]{4,3,2,1,0:T(8,128)} fusion(bf16[1,8,8,8,1024]{4,3,2,1,0:T(8,128)(2,1)S(1)} %bitcast.87, bf16[1,8,8,8,1024]{4,3,2,1,0:T(8,128)(2,1)S(1)} %bitcast.85), kind=kLoop, calls=%fused_computation.17 | loop fusion | flops 2097152 | bytes 6291456 | tf_op jit(solution)/shard_map/convert_element_type | solution.py:32
  61.9 7.0 %fusion.22 = (f32[128]{0:T(128)S(1)}, f32[128,624]{0,1:T(8,128)S(1)}) fusion(s32[128]{0:T(128)S(1)} %eq.29, s32[624]{0:T(1024)S(1)} %iota_add_fusion, pred[624]{0:T(1024)(128)(4,1)S(1)} %broadcast_compare_fusion, bf16[624,8192]{1,0:T(8,128)(2,1)} %param.7, f32[128,8192]{1,0:T(8,128)} %bitcast.81, f32[8192]{0:T(1024)S(1)} %copy-done.3, f32[128]{0:T(128)S(1)} %rsqrt.11), kind=kOutput, calls=%fused_computation.35 | convolution fusion | flops 1312087936 | bytes 14774832 | tf_op jit(solution)/shard_map/td,vd->tv/dot_general | solution.py:35
  69.5 2.0 %collective-permute-start.1 = (f32[4,2,64]{2,1,0:T(2,128)S(1)}, f32[4,2,64]{2,1,0:T(2,128)S(1)}, u32[]{:S(2)}, u32[]{:S(2)}) collective-permute-start(f32[4,2,64]{2,1,0:T(2,128)S(1)} %rev.7), channel_id=1, source_target_pairs={{0,8},{8,0},{1,9},{9,1},{2,10},{10,2},{3,11},{11,3},{4,12},{12,4},... | collective-permute-start | bytes 6152 | tf_op jit(solution)/shard_map/ppermute | solution.py:14
  71.6 1.0 collective-permute-done.1
  72.7 0.7 broadcast_in_dim.18
  73.4 6.4 %all-to-all-start.1 = ((f32[64,4,128]{2,1,0:T(4,128)}), f32[64,4,128]{2,1,0:T(4,128)S(1)}, u32[]{:S(2)}, u32[]{:S(2)}) async-start(f32[64,4,128]{2,1,0:T(4,128)} %broadcast_in_dim.18), calls=%async_computation.1 | async-start | bytes 262144 | tf_op jit(solution)/shard_map/all_to_all | solution.py:63
  79.8 7.2 %fusion.16 = bf16[128,8,1024]{2,0,1:T(8,128)(2,1)} fusion(bf16[78,8,8,1024]{3,2,1,0:T(8,128)(2,1)} %bitcast.82, s32[128]{0:T(128)S(1)} %eq.29, s32[624]{0:T(1024)S(1)} %iota_add_fusion), kind=kOutput, calls=%fused_computation.27 | convolution fusion | flops 1309751296 | bytes 12323776 | tf_op jit(solution)/shard_map/tv,vkd->tkd/dot_general | solution.py:71
  87.0 5.7 %all-to-all-done.1 = f32[64,4,128]{2,1,0:T(4,128)S(1)} async-done(((f32[64,4,128]{2,1,0:T(4,128)}), f32[64,4,128]{2,1,0:T(4,128)S(1)}, u32[]{:S(2)}, u32[]{:S(2)}) %all-to-all-start.1) | async-done | bytes 131104 | tf_op jit(solution)/shard_map/all_to_all | solution.py:63
  92.9 6.1 %multiply_convert_fusion = bf16[128,8,1024]{2,0,1:T(8,128)(2,1)S(1)} fusion(f32[128]{0:T(128)S(1)} %get-tuple-element.23, bf16[78,8,8,1024]{3,2,1,0:T(8,128)(2,1)} %bitcast.83, f32[128,624]{0,1:T(8,128)S(1)} %get-tuple-element.25, f32[128]{0:T(128)S(1)} %get-tuple-element.24, s32[128]{0:T(128)S(1)} %eq.29, s32[624]{0:T(1024)S(1)} %iota_add_fusion, ...), kind=kOutput, calls=%fused_computation.9 | convolution fusion | flops 1311199232 | bytes 12644912 | tf_op jit(solution)/shard_map/tv,vkd->tkd/dot_general | solution.py:71
  99.5 1.6 %fusion.9 = bf16[2,8,8,8,1024]{4,3,2,1,0:T(8,128)(2,1)} fusion(bf16[2,1,8,8,8,1024]{5,4,3,2,1,0:T(8,128)(2,1)S(1)} %get-tuple-element.26, bf16[2,1,8,8,8,1024]{5,4,3,2,1,0:T(8,128)(2,1)S(1)} %get-tuple-element.27), kind=kLoop, calls=%fused_computation.16 | loop fusion | flops 1048576 | bytes 6291456 | tf_op jit(solution)/shard_map/squeeze | solution.py:78
  101.5 1.9 %collective-permute-start.2 = (bf16[2,8,8,8,1024]{4,3,2,1,0:T(8,128)(2,1)}, bf16[2,8,8,8,1024]{4,3,2,1,0:T(8,128)(2,1)}, u32[]{:S(2)}, u32[]{:S(2)}) collective-permute-start(bf16[2,8,8,8,1024]{4,3,2,1,0:T(8,128)(2,1)} %fusion.9), channel_id=1, source_target_pairs={{0,8},{8,0},{1,9},{9,1},{2,10},{10,2},{3,11},{11,3},{4,12},{12,4},... | collective-permute-start | bytes 6291464 | tf_op jit(solution)/shard_map/ppermute | solution.py:14
  103.6 4.3 %collective-permute-done.2 = bf16[2,8,8,8,1024]{4,3,2,1,0:T(8,128)(2,1)} collective-permute-done((bf16[2,8,8,8,1024]{4,3,2,1,0:T(8,128)(2,1)}, bf16[2,8,8,8,1024]{4,3,2,1,0:T(8,128)(2,1)}, u32[]{:S(2)}, u32[]{:S(2)}) %collective-permute-start.2) | collective-permute-done | bytes 2097184 | tf_op jit(solution)/shard_map/ppermute | solution.py:14
  107.9 2.8 %convert_add_fusion = f32[2,8,8,8,1024]{4,3,2,1,0:T(8,128)S(1)} fusion(bf16[2,8,8,8,1024]{4,3,2,1,0:T(8,128)(2,1)} %collective-permute-done.2, bf16[2,1,8,8,8,1024]{5,4,3,2,1,0:T(8,128)(2,1)} %copy-done, bf16[2,1,8,8,8,1024]{5,4,3,2,1,0:T(8,128)(2,1)S(1)} %get-tuple-element.26), kind=kLoop, calls=%fused_computation.8 | loop fusion | flops 4194304 | bytes 10485760 | tf_op jit(solution)/shard_map/add | solution.py:78
  110.6 0.6 fusion.41
  111.2 1.3 fusion.11
  112.5 7.2 %all-to-all-start.2 = ((bf16[64,8,1024]{2,1,0:T(8,128)(2,1)}), bf16[64,8,1024]{2,1,0:T(8,128)(2,1)S(1)}, u32[]{:S(2)}, u32[]{:S(2)}) async-start(bf16[64,8,1024]{2,1,0:T(8,128)(2,1)} %fusion.11), calls=%async_computation.2 | async-start | bytes 2097152 | tf_op jit(solution)/shard_map/all_to_all | solution.py:91
  119.9 0.6 dynamic_slice.12
  120.5 29.1 %all-to-all-done.2 = bf16[64,8,1024]{2,1,0:T(8,128)(2,1)S(1)} async-done(((bf16[64,8,1024]{2,1,0:T(8,128)(2,1)}), bf16[64,8,1024]{2,1,0:T(8,128)(2,1)S(1)}, u32[]{:S(2)}, u32[]{:S(2)}) %all-to-all-start.2) | async-done | bytes 1048608 | tf_op jit(solution)/shard_map/all_to_all | solution.py:91
  149.8 0.7 multiply_convert_fusion.3
  (48 shorter events, 2.6 us)
Async XLA Ops:
  0.6 55.8 %copy-start.5 = (s32[128]{0:T(128)S(1)}, s32[128]{0:T(128)}, u32[]{:S(2)}) copy-start(s32[128]{0:T(128)} %param.8) | copy-start | bytes 1540
  0.6 56.1 %copy-start.4 = (s32[624]{0:T(1024)S(1)}, s32[624]{0:T(1024)}, u32[]{:S(2)}) copy-start(s32[624]{0:T(1024)} %param.9) | copy-start | bytes 7492
  54.5 4.5 %collective-permute-start = (bf16[64,8,1024]{2,1,0:T(8,128)(2,1)S(1)}, bf16[64,8,1024]{2,1,0:T(8,128)(2,1)S(1)}, u32[]{:S(2)}, u32[]{:S(2)}) collective-permute-start(bf16[64,8,1024]{2,1,0:T(8,128)(2,1)S(1)} %all_to_all.15), channel_id=1, source_target_pairs={{0,8},{8,0},{1,9},{9,1},{2,10},{10,2},{3,11},{11,3},{4,12},{12,4},... | collective-permute-start | bytes 3145736 | tf_op jit(solution)/shard_map/ppermute | solution.py:14
  59.6 2.3 %copy-start.3 = (f32[8192]{0:T(1024)S(1)}, f32[8192]{0:T(1024)}, u32[]{:S(2)}) copy-start(f32[8192]{0:T(1024)} %param.6) | copy-start | bytes 98308
  69.5 3.1 %collective-permute-start.1 = (f32[4,2,64]{2,1,0:T(2,128)S(1)}, f32[4,2,64]{2,1,0:T(2,128)S(1)}, u32[]{:S(2)}, u32[]{:S(2)}) collective-permute-start(f32[4,2,64]{2,1,0:T(2,128)S(1)} %rev.7), channel_id=1, source_target_pairs={{0,8},{8,0},{1,9},{9,1},{2,10},{10,2},{3,11},{11,3},{4,12},{12,4},... | collective-permute-start | bytes 6152 | tf_op jit(solution)/shard_map/ppermute | solution.py:14
  73.4 19.3 %all-to-all-start.1 = ((f32[64,4,128]{2,1,0:T(4,128)}), f32[64,4,128]{2,1,0:T(4,128)S(1)}, u32[]{:S(2)}, u32[]{:S(2)}) async-start(f32[64,4,128]{2,1,0:T(4,128)} %broadcast_in_dim.18), calls=%async_computation.1 | async-start | bytes 262144 | tf_op jit(solution)/shard_map/all_to_all | solution.py:63
  92.9 6.1 %copy-start.1 = (bf16[128,8,1024]{2,0,1:T(8,128)(2,1)S(1)}, bf16[128,8,1024]{2,0,1:T(8,128)(2,1)}, u32[]{:S(2)}) copy-start(bf16[128,8,1024]{2,0,1:T(8,128)(2,1)} %fusion.16) | copy-start | bytes 6291460
  99.5 2.0 %copy-start = (bf16[2,1,8,8,8,1024]{5,4,3,2,1,0:T(8,128)(2,1)}, bf16[2,1,8,8,8,1024]{5,4,3,2,1,0:T(8,128)(2,1)S(1)}, u32[]{:S(2)}) copy-start(bf16[2,1,8,8,8,1024]{5,4,3,2,1,0:T(8,128)(2,1)S(1)} %get-tuple-element.27) | copy-start | bytes 6291460
  101.5 6.4 %collective-permute-start.2 = (bf16[2,8,8,8,1024]{4,3,2,1,0:T(8,128)(2,1)}, bf16[2,8,8,8,1024]{4,3,2,1,0:T(8,128)(2,1)}, u32[]{:S(2)}, u32[]{:S(2)}) collective-permute-start(bf16[2,8,8,8,1024]{4,3,2,1,0:T(8,128)(2,1)} %fusion.9), channel_id=1, source_target_pairs={{0,8},{8,0},{1,9},{9,1},{2,10},{10,2},{3,11},{11,3},{4,12},{12,4},... | collective-permute-start | bytes 6291464 | tf_op jit(solution)/shard_map/ppermute | solution.py:14
  112.5 37.2 %copy-start.2 = (bf16[8,1024]{1,0:T(8,128)(2,1)S(1)}, bf16[8,1024]{1,0:T(8,128)(2,1)}, u32[]{:S(2)}) copy-start(bf16[8,1024]{1,0:T(8,128)(2,1)} %param.5) | copy-start | bytes 49156
  112.5 37.1 %all-to-all-start.2 = ((bf16[64,8,1024]{2,1,0:T(8,128)(2,1)}), bf16[64,8,1024]{2,1,0:T(8,128)(2,1)S(1)}, u32[]{:S(2)}, u32[]{:S(2)}) async-start(bf16[64,8,1024]{2,1,0:T(8,128)(2,1)} %fusion.11), calls=%async_computation.2 | async-start | bytes 2097152 | tf_op jit(solution)/shard_map/all_to_all | solution.py:91

commit v2 on v1

v2 whole, which is shorter than its diff:
```python
import functools
import jax
import jax.numpy as jnp
from jax import lax
from jax.experimental import pallas as pl
from jax.experimental.pallas import tpu as pltpu
from jax.sharding import Mesh
from jax.sharding import PartitionSpec as P

EPSILON = 1e-05
LOWEST = -1e30
CORES = 2
PLANE = ("z", "tensor")
MIB = 1 << 20


def swap_cores(values):
    return lax.ppermute(values, "core", [(0, 1), (1, 0)])


def head_copy(head_ref, chunk_ref, semaphores, y, width):
    columns = pl.ds(pl.multiple_of(y * width, width), width)
    return pltpu.make_async_copy(head_ref.at[:, columns], chunk_ref.at[:, columns], semaphores.at[y])


def swap_halves(row):
    half = row.shape[1] // 2
    return jnp.concatenate([row[:, half:], row[:, :half]], axis=1)


def to_column(row):
    n = row.shape[1]
    square = jnp.broadcast_to(row, (n, n))
    here = lax.broadcasted_iota(jnp.int32, (n, n), 0) == lax.broadcasted_iota(jnp.int32, (n, n), 1)
    return jnp.sum(jnp.where(here, square, 0.0), axis=1, keepdims=True)


def logits_kernel(start_ref, got_ref, swapped_ref, gain_ref, head_ref, targets_ref, banned_ref,
                  lefts_ref, stats_ref, inverse_ref, normed_ref, logits_ref, chunk_ref, semaphores, *, n_z, n_y):
    k, width = got_ref.shape[1:]
    tokens, full_width = normed_ref.shape
    vocab_rows = head_ref.shape[0]
    for y in range(n_y):
        head_copy(head_ref, chunk_ref, semaphores, y, width).start()

    for slot, source in enumerate((got_ref, swapped_ref)):

        @pl.loop(0, n_z // 2)
        def _(pair, slot=slot, source=source):
            first = pair * 2 * n_y
            total = jnp.zeros((2 * k, width), jnp.float32)
            for y in range(n_y):
                block = jnp.concatenate([source[first + y], source[first + n_y + y]], axis=0).astype(jnp.float32)
                total = total + block * block
            inverse = lax.rsqrt(jnp.sum(total, axis=1, keepdims=True) / full_width + EPSILON)
            row = pl.multiple_of(slot * (tokens // 2) + pair * 2 * k, 2 * k)
            inverse_ref[pl.ds(row, 2 * k), :] = jnp.broadcast_to(inverse, (2 * k, inverse_ref.shape[1]))
            for y in range(n_y):
                block = jnp.concatenate([source[first + y], source[first + n_y + y]], axis=0).astype(jnp.float32)
                columns = pl.ds(y * width, width)
                normed_ref[pl.ds(row, 2 * k), columns] = (block * inverse * gain_ref[:, columns]).astype(jnp.bfloat16)

    logits_ref[...] = jnp.zeros_like(logits_ref)

    @pl.loop(0, n_y)
    def _(y):
        head_copy(head_ref, chunk_ref, semaphores, y, width).wait()
        columns = pl.ds(pl.multiple_of(y * width, width), width)
        logits_ref[...] += lax.dot_general(
            chunk_ref[:, columns], normed_ref[:, columns], (((1,), (1,)), ((), ())),
            preferred_element_type=jnp.float32)

    logits = logits_ref[...]
    ids = start_ref[0] + lax.broadcasted_iota(jnp.int32, (vocab_rows, tokens), 0)
    is_target = ids == targets_ref[...]
    allowed = (banned_ref[...] == 0) | is_target
    top = jnp.max(jnp.where(allowed, logits, LOWEST), axis=0, keepdims=True)
    below = logits - top
    shifted = jnp.where(allowed, jnp.exp(below), 0.0)
    total = jnp.sum(shifted, axis=0, keepdims=True)
    dot = jnp.sum(jnp.where(allowed, shifted * below, 0.0), axis=0, keepdims=True)
    target_logit = jnp.sum(jnp.where(is_target, logits, 0.0), axis=0, keepdims=True)
    for i, row in enumerate((top, total, dot, target_logit)):
        stats_ref[0, i : i + 1, :] = row
        stats_ref[1, i : i + 1, :] = swap_halves(row)
    lefts_ref[0] = jnp.where(is_target, 0.0, shifted).T.astype(jnp.bfloat16)
    lefts_ref[1] = is_target.astype(jnp.float32).T.astype(jnp.bfloat16)


def pair_kernel(mine_ref, theirs_ref, out_ref):
    mine, theirs = mine_ref[0], theirs_ref[...]
    top = jnp.maximum(mine[0:1], theirs[0:1])
    total, dot = 0.0, 0.0
    for part in (mine, theirs):
        gap = part[0:1] - top
        weight = jnp.exp(gap)
        total = total + weight * part[1:2]
        dot = dot + weight * (part[2:3] + part[1:2] * gap)
    pair = jnp.concatenate([top, total, dot, mine[3:4] + theirs[3:4]], axis=0)
    out_ref[...] = jnp.broadcast_to(pair[None], out_ref.shape)


def terms_kernel(mine_ref, pair_ref, lefts_ref, head_ref, terms_ref, picks_ref, chunk_ref, semaphores,
                 *, n_z, n_y, slot):
    k, width = picks_ref.shape[-2:]
    half = lefts_ref.shape[1] // 2
    for y in range(n_y):
        head_copy(head_ref, chunk_ref, semaphores, y, width).start()
    here = slice(slot * half, (slot + 1) * half)
    share = to_column(jnp.exp(mine_ref[0, 0:1, :] - pair_ref[0, 0:1, :]))[here]
    lefts = jnp.concatenate([lefts_ref[0, here], lefts_ref[1, here]], axis=0)

    @pl.loop(0, n_y)
    def _(y):
        head_copy(head_ref, chunk_ref, semaphores, y, width).wait()
        columns = pl.ds(pl.multiple_of(y * width, width), width)
        terms = jnp.dot(lefts, chunk_ref[:, columns], preferred_element_type=jnp.float32)
        scaled = terms[:half] * share
        for z in range(n_z):
            rows = slice(z * k, (z + 1) * k)
            terms_ref[z * n_y + y] = scaled[rows].astype(terms_ref.dtype)
            picks_ref[z * n_y + y] = terms[half:][rows].astype(picks_ref.dtype)


def send_kernel(mine_ref, pair_ref, lefts_ref, head_ref, send_ref, chunk_ref, semaphores, *, n_z, n_y):
    terms_kernel(mine_ref, pair_ref, lefts_ref, head_ref, send_ref.at[0], send_ref.at[1], chunk_ref, semaphores,
                 n_z=n_z, n_y=n_y, slot=1)


def keep_kernel(mine_ref, pair_ref, lefts_ref, head_ref, keep_ref, keep_picks_ref, chunk_ref, semaphores, *, n_z, n_y):
    terms_kernel(mine_ref, pair_ref, lefts_ref, head_ref, keep_ref, keep_picks_ref, chunk_ref, semaphores,
                 n_z=n_z, n_y=n_y, slot=0)


def combine_kernel(pair_ref, everyone_ref, loss_ref, columns_ref, *, full_width):
    everyone = everyone_ref[...]
    maxima, sums, dots = everyone[:, 0, :], everyone[:, 1, :], everyone[:, 2, :]
    top = jnp.max(maxima, axis=0, keepdims=True)
    gap = maxima - top
    weight = jnp.exp(gap)
    total = jnp.sum(weight * sums, axis=0, keepdims=True)
    dot = jnp.sum(weight * (dots + sums * gap), axis=0, keepdims=True)
    target_logit = jnp.sum(everyone[:, 3, :], axis=0, keepdims=True)
    loss_ref[...] = jnp.broadcast_to(top + jnp.log(total) - target_logit, loss_ref.shape)
    inner = (dot / total - (target_logit - top)) / full_width
    scale = jnp.exp(pair_ref[0, 0:1, :] - top) / total
    target_scale = (jnp.exp(target_logit - top) / total - 1.0).astype(jnp.bfloat16).astype(jnp.float32)
    lane = lax.broadcasted_iota(jnp.int32, columns_ref.shape, 1)
    columns = jnp.where(lane == 1, to_column(target_scale), to_column(inner))
    columns_ref[...] = jnp.where(lane == 0, to_column(scale), columns)


def pieces_kernel(columns_ref, keep_ref, keep_picks_ref, received_ref, pieces_ref, *, n_z, n_y):
    k, width = keep_ref.shape[1:]

    @pl.loop(0, n_z)
    def _(z):
        rows = pl.ds(pl.multiple_of(z * k, k), k)
        rows_scale = jnp.broadcast_to(columns_ref[rows, 0:1], (k, width))
        picks_scale = jnp.broadcast_to(columns_ref[rows, 1:2], (k, width))
        for y in range(n_y):
            i = z * n_y + y
            terms = keep_ref[i] + received_ref[0, i].astype(jnp.float32)
            picks = keep_picks_ref[i].astype(jnp.float32) + received_ref[1, i].astype(jnp.float32)
            pieces_ref[i] = (terms * rows_scale + picks * picks_scale).astype(jnp.bfloat16)


VMEM = pl.BlockSpec(memory_space=pltpu.VMEM)
HBM = pl.BlockSpec(memory_space=pltpu.HBM)
SMEM = pl.BlockSpec(memory_space=pltpu.SMEM)


def local(hidden, gain, lm_head, targets, banned):
    z_count = lax.axis_size("z")
    tensor_count = lax.axis_size("tensor")
    chips = z_count * tensor_count
    z_index = lax.axis_index("z")
    core_index = lax.axis_index("core")
    tensor_index = lax.axis_index("tensor")
    own_tokens, own_width = hidden.shape
    vocab_rows, full_width = lm_head.shape
    tokens = targets.shape[0]
    f32, bf16 = jnp.float32, jnp.bfloat16
    struct = jax.ShapeDtypeStruct
    head = pltpu.with_memory_space_constraint(lm_head, pltpu.HBM)
    head_scratch = [pltpu.VMEM(lm_head.shape, bf16), pltpu.SemaphoreType.DMA((tensor_count,))]

    by_core = targets.reshape(z_count, CORES, own_tokens)
    row_targets = jnp.where(core_index == 0, by_core, by_core[:, ::-1]).transpose(1, 0, 2).reshape(1, tokens)
    vocab_start = ((z_index * CORES + core_index) * tensor_count + tensor_index) * vocab_rows
    banned_rows = jnp.broadcast_to(banned[:, None], (vocab_rows, tokens))

    sent = jnp.broadcast_to(hidden[None], (chips, own_tokens, own_width))
    got = lax.all_to_all(sent, PLANE, 0, 0, tiled=True)
    swapped = swap_cores(got)

    matmul_flops = 2 * tokens * vocab_rows * full_width
    lefts, mine, inverse = pl.pallas_call(
        functools.partial(logits_kernel, n_z=z_count, n_y=tensor_count),
        out_shape=(struct((2, tokens, vocab_rows), bf16), struct((2, 4, tokens), f32), struct((tokens, 128), f32)),
        in_specs=[SMEM, VMEM, VMEM, VMEM, HBM, VMEM, VMEM],
        out_specs=(VMEM,) * 3,
        scratch_shapes=[pltpu.VMEM((tokens, full_width), bf16), pltpu.VMEM((vocab_rows, tokens), f32)] + head_scratch,
        compiler_params=pltpu.CompilerParams(vmem_limit_bytes=32 * MIB),
        cost_estimate=pl.CostEstimate(flops=matmul_flops, bytes_accessed=12 * MIB, transcendentals=tokens * vocab_rows),
        name="logits",
    )(vocab_start.reshape(1), got, swapped, gain.reshape(1, full_width), head, row_targets, banned_rows)

    theirs = swap_cores(mine[1])
    pair = pl.pallas_call(
        pair_kernel, out_shape=struct((chips, 4, tokens), f32), in_specs=[VMEM] * 2, out_specs=VMEM,
        compiler_params=pltpu.CompilerParams(vmem_limit_bytes=2 * MIB), name="pair",
    )(mine, theirs)
    everyone = lax.all_to_all(pair, PLANE, 0, 0, tiled=True)

    piece = (chips, own_tokens, own_width)
    def half_terms(kernel, out_shape, weight, name):
        return pl.pallas_call(
            functools.partial(kernel, n_z=z_count, n_y=tensor_count),
            out_shape=out_shape,
            in_specs=[VMEM, VMEM, VMEM, HBM],
            out_specs=jax.tree.map(lambda _: VMEM, out_shape),
            scratch_shapes=head_scratch,
            compiler_params=pltpu.CompilerParams(vmem_limit_bytes=32 * MIB),
            cost_estimate=pl.CostEstimate(
                flops=weight * matmul_flops, bytes_accessed=weight * 13 * MIB, transcendentals=0),
            name=name,
        )(mine, pair, lefts, head)

    send = half_terms(send_kernel, struct((2,) + piece, bf16), 1, "send")
    received = swap_cores(send)
    keep, keep_picks = half_terms(keep_kernel, (struct(piece, f32), struct(piece, bf16)), 100, "keep")

    loss, columns = pl.pallas_call(
        functools.partial(combine_kernel, full_width=full_width),
        out_shape=(struct((8, tokens), f32), struct((tokens, 128), f32)),
        in_specs=[VMEM] * 2,
        out_specs=(VMEM,) * 2,
        compiler_params=pltpu.CompilerParams(vmem_limit_bytes=4 * MIB),
        cost_estimate=pl.CostEstimate(flops=0, bytes_accessed=32 * MIB, transcendentals=0),
        name="combine",
    )(pair, everyone)
    pieces = pl.pallas_call(
        functools.partial(pieces_kernel, n_z=z_count, n_y=tensor_count),
        out_shape=struct(piece, bf16),
        in_specs=[VMEM] * 4,
        out_specs=VMEM,
        compiler_params=pltpu.CompilerParams(vmem_limit_bytes=16 * MIB),
        cost_estimate=pl.CostEstimate(flops=0, bytes_accessed=8 * MIB, transcendentals=0),
        name="pieces",
    )(columns, keep, keep_picks, received)
    grad_normed = jnp.sum(lax.all_to_all(pieces, PLANE, 0, 0, tiled=True).astype(f32), axis=0)

    def own_rows(values):
        return lax.dynamic_slice_in_dim(values, z_index * own_tokens, own_tokens)

    gain_own = lax.dynamic_slice_in_dim(gain, tensor_index * own_width, own_width)
    inverse_own = own_rows(inverse)[:, :1]
    scaled = hidden.astype(f32) * inverse_own
    gated = grad_normed * gain_own[None, :]
    grad_hidden = (inverse_own * (gated - scaled * own_rows(columns)[:, 2:3])).astype(bf16)
    return (own_rows(loss[0]), grad_hidden)


def solution(mesh):
    dp, pipe, tensor = mesh.devices.shape
    fine = Mesh(mesh.devices.reshape(dp, pipe // CORES, CORES, tensor), ("dp", "z", "core", "tensor"))
    section = ("dp", "z", "core")
    in_specs = (
        P(section, "tensor"),
        P(),
        P(("z", "core", "tensor"), None),
        P("dp"),
        P(("z", "core", "tensor")),
    )
    out_specs = (P(section), P(section, "tensor"))
    return jax.shard_map(local, mesh=fine, in_specs=in_specs, out_specs=out_specs, check_vma=False)
```

time: 151 us -> 141 us (0.934)
  Pallas kernels: 0 us -> 21.8 us
  matrix products: 20.4 us -> 0 us
  waiting for transfers between devices: 42.4 us -> 32.8 us
  other arithmetic: 9.74 us -> 0.87 us
  starting transfers between devices: 19.4 us -> 25.1 us
    pallas_call x0 -> x6, Pallas kernels: none -> 21.8 us  [the longest x2 12.1 us: half_terms(): pl.pallas_call(functools.partial(kernel, n_z=z_count, n_y=tensor_count),...]
    dot_general x3 -> x0, matrix products: 20.4 us -> none  [the longest x2 13.3 us: split_terms(): jnp.einsum('tv,vkd->tkd', left, head_split, preferred_element_type=jnp.fl...]
    all_to_all x2, starting transfers between devices: 13.6 us -> 19.3 us  [the longest x1 12.8 us: local(): lax.all_to_all(pieces, PLANE, 0, 0, tiled=True).astype(f32)]
    all_to_all x2, waiting for transfers between devices: 34.8 us -> 29.5 us  [the longest x1 29.5 us: local(): lax.all_to_all(pieces, PLANE, 0, 0, tiled=True).astype(f32)]
    ppermute x3, waiting for transfers between devices: 7.59 us -> 3.35 us  [swap_cores(): return lax.ppermute(values, 'core', [(0, 1), (1, 0)])]
    unnamed x12 -> x16, local copies, waits for them, and re-layouts: 0.35 us -> 3.89 us
    convert_element_type x3 -> x1, other arithmetic: 4.19 us -> 0.68 us  [local(): (inverse_own * (gated - scaled * own_rows(columns)[:, 2:3])).astype(bf16)]
    add x2 -> x0, other arithmetic: 2.76 us -> none  [the longest x1 2.75 us: local(): terms[0].astype(jnp.float32) + swap_cores(terms[1]).astype(jnp.float32)]
  transfers between devices with their start and end apart: 5 -> 5, of which waited for: 5 -> 3; matrix products, arithmetic and copies ran while one was open for 6% -> 1% of each run, Pallas kernels for 0% -> 5%
where the time goes in v2:
time: 141 us; the launch traced here: 140 us
  blocking collectives  53 us (38%)
  waiting for transfers between devices  32.8 us (23%)
  starting transfers between devices  25.1 us (18%)
  Pallas kernels  21.8 us (15%)
  local copies, waits for them, and re-layouts  5.88 us (4%)
    all_to_all x1, blocking collectives, local(): got = lax.all_to_all(sent, PLANE, 0, 0, tiled=True)  53 us
    all_to_all x1, waiting for transfers between devices, local(): lax.all_to_all(pieces, PLANE, 0, 0, tiled=True).astype(f32)  29.5 us
    all_to_all x1, starting transfers between devices, local(): lax.all_to_all(pieces, PLANE, 0, 0, tiled=True).astype(f32)  12.8 us
    pallas_call x2, Pallas kernels, half_terms(): pl.pallas_call(functools.partial(kernel, n_z=z_count, n_y=tensor_count),...  12.1 us
    all_to_all x1, starting transfers between devices, local(): everyone = lax.all_to_all(pair, PLANE, 0, 0, tiled=True)  6.42 us
    pallas_call x1, Pallas kernels, local(): pl.pallas_call(functools.partial(logits_kernel, n_z=z_count, n_y=tensor_c...  6.19 us
    ppermute x3, starting transfers between devices, swap_cores(): return lax.ppermute(values, 'core', [(0, 1), (1, 0)])  5.87 us
    unnamed x16, local copies, waits for them, and re-layouts  3.89 us
  transfers between devices with their start and end apart: 5, of which 3 were waited for; matrix products, arithmetic and copies ran while one was open for 1% of the time, Pallas kernels for 5%

profile of v2, /device:TPU:14, one launch (start us, length us, event | category | flops | bytes accessed | tf_op | source)
XLA Modules:
  0.0 140.4 jit_solution(16539309648677243232)
XLA Ops:
  0.7 0.8 broadcast_in_dim.4
  1.5 53.0 %all_to_all.15.got_ref = bf16[64,8,1024]{2,1,0:T(8,128)(2,1)S(1)} all-to-all(bf16[64,8,1024]{2,1,0:T(8,128)(2,1)S(1)} %broadcast_in_dim.4), channel_id=1, replica_groups=mesh['dp'=8,'z'=8,'core'=2,'tensor'=8] {'z','tensor'}, dimensions={0} | all-to-all | bytes 2097152 | tf_op jit(solution)/shard_map/all_to_all | solution.py:194
  54.5 1.9 %collective-permute-start = (bf16[64,8,1024]{2,1,0:T(8,128)(2,1)S(1)}, bf16[64,8,1024]{2,1,0:T(8,128)(2,1)S(1)}, u32[]{:S(2)}, u32[]{:S(2)}) collective-permute-start(bf16[64,8,1024]{2,1,0:T(8,128)(2,1)S(1)} %all_to_all.15.got_ref), channel_id=1, source_target_pairs={{0,8},{8,0},{1,9},{9,1},{2,10},{10,2},{3,11},{11,3},{4,12},{12,4},... | collective-permute-start | bytes 3145736 | tf_op jit(solution)/shard_map/ppermute | solution.py:18
  56.7 2.3 %collective-permute-done.swapped_ref = bf16[64,8,1024]{2,1,0:T(8,128)(2,1)S(1)} collective-permute-done((bf16[64,8,1024]{2,1,0:T(8,128)(2,1)S(1)}, bf16[64,8,1024]{2,1,0:T(8,128)(2,1)S(1)}, u32[]{:S(2)}, u32[]{:S(2)}) %collective-permute-start) | collective-permute-done | bytes 1048608 | tf_op jit(solution)/shard_map/ppermute | solution.py:18
  59.1 0.1 broadcast_in_dim.5.banned_ref
  59.2 6.2 %logits.1 = (bf16[2,128,624]{2,1,0:T(8,128)(2,1)S(1)}, f32[2,4,128]{2,1,0:T(4,128)S(1)}, f32[128,128]{1,0:T(8,128)S(1)}) custom-call(s32[1]{0:T(128)} %bitcast.start_ref, bf16[64,8,1024]{2,1,0:T(8,128)(2,1)S(1)} %all_to_all.15.got_ref, bf16[64,8,1024]{2,1,0:T(8,128)(2,1)S(1)} %collective-permute-done.swapped_ref, f32[1,8192]{1,0:T(1,128)S(1)} %bitcast.8, ...), custom_call_target="tpu_custom_call" | custom-call | flops 1308622848 | bytes 12582912 | tf_op jit(solution)/shard_map/logits/pallas_call | solution.py:198
  65.4 2.0 %collective-permute-start.1 = (f32[4,128]{1,0:T(4,128)S(1)}, f32[4,128]{1,0:T(4,128)S(1)}, u32[]{:S(2)}, u32[]{:S(2)}) collective-permute-start(f32[4,128]{1,0:T(4,128)S(1)} %slice_bitcast_fusion), channel_id=1, source_target_pairs={{0,8},{8,0},{1,9},{9,1},{2,10},{10,2},{3,11},{11,3},{4,12},{12,4},... | collective-permute-start | bytes 6152 | tf_op jit(solution)/shard_map/ppermute | solution.py:18
  67.5 1.0 collective-permute-done.1.theirs_ref
  68.5 0.7 pair.1.pair_ref
  69.2 6.4 %all-to-all-start.1 = ((f32[64,4,128]{2,1,0:T(4,128)}), f32[64,4,128]{2,1,0:T(4,128)S(1)}, u32[]{:S(2)}, u32[]{:S(2)}) async-start(f32[64,4,128]{2,1,0:T(4,128)} %pair.1.pair_ref), calls=%async_computation.1 | async-start | bytes 262144 | tf_op jit(solution)/shard_map/all_to_all | solution.py:214
  75.6 6.7 %send.1 = bf16[2,64,8,1024]{3,2,1,0:T(8,128)(2,1)} custom-call(f32[2,4,128]{2,1,0:T(4,128)S(1)} %get-tuple-element.9.mine_ref, f32[64,4,128]{2,1,0:T(4,128)} %pair.1.pair_ref, bf16[2,128,624]{2,1,0:T(8,128)(2,1)S(1)} %get-tuple-element.13.lefts_ref, bf16[624,8192]{1,0:T(8,128)(2,1)} %head_ref.5), custom_call_target="tpu_custom_call" | custom-call | flops 1308622848 | bytes 13631488 | tf_op jit(solution)/shard_map/send/pallas_call | solution.py:218
  82.3 1.9 %collective-permute-start.2 = (bf16[2,64,8,1024]{3,2,1,0:T(8,128)(2,1)}, bf16[2,64,8,1024]{3,2,1,0:T(8,128)(2,1)S(1)}, u32[]{:S(2)}, u32[]{:S(2)}) collective-permute-start(bf16[2,64,8,1024]{3,2,1,0:T(8,128)(2,1)} %send.1), channel_id=1, source_target_pairs={{0,8},{8,0},{1,9},{9,1},{2,10},{10,2},{3,11},{11,3},{4,12},{12,4},... | collective-permute-start | bytes 6291464 | tf_op jit(solution)/shard_map/ppermute | solution.py:18
  84.2 1.0 copy-done.3
  85.2 5.3 %keep.1 = (f32[64,8,1024]{2,1,0:T(8,128)S(1)}, bf16[64,8,1024]{2,1,0:T(8,128)(2,1)S(1)}) custom-call(f32[2,4,128]{2,1,0:T(4,128)S(1)} %get-tuple-element.9.mine_ref, f32[64,4,128]{2,1,0:T(4,128)} %pair.1.pair_ref, bf16[2,128,624]{2,1,0:T(8,128)(2,1)S(1)} %copy-done.3, bf16[624,8192]{1,0:T(8,128)(2,1)} %head_ref.5), custom_call_target="tpu_custom_call" | custom-call | flops 130862284800 | bytes 1363148800 | tf_op jit(solution)/shard_map/keep/pallas_call | solution.py:218
  90.6 1.3 copy-done
  91.9 1.1 combine.1
  93.1 1.6 %copy-done.1 = f32[64,8,1024]{2,1,0:T(8,128)S(1)} copy-done((f32[64,8,1024]{2,1,0:T(8,128)S(1)}, f32[64,8,1024]{2,1,0:T(8,128)}, u32[]{:S(2)}) %copy-start.1) | copy-done | bytes 2097176
  94.6 1.8 %pieces.1 = bf16[64,8,1024]{2,1,0:T(8,128)(2,1)} custom-call(f32[128,128]{1,0:T(8,128)S(1)} %get-tuple-element.12.columns_ref, f32[64,8,1024]{2,1,0:T(8,128)S(1)} %copy-done.1, bf16[64,8,1024]{2,1,0:T(8,128)(2,1)S(1)} %get-tuple-element.15.keep_picks_ref, bf16[2,64,8,1024]{3,2,1,0:T(8,128)(2,1)S(1)} %collective-permute-done.2.received_ref), custom_call_target="tpu_custom_call" | custom-call | bytes 8388608 | tf_op jit(solution)/shard_map/pieces/pallas_call | solution.py:243
  96.4 12.8 %all-to-all-start.2 = ((bf16[64,8,1024]{2,1,0:T(8,128)(2,1)}), bf16[64,8,1024]{2,1,0:T(8,128)(2,1)S(1)}, u32[]{:S(2)}, u32[]{:S(2)}) async-start(bf16[64,8,1024]{2,1,0:T(8,128)(2,1)} %pieces.1), calls=%async_computation.2 | async-start | bytes 2097152 | tf_op jit(solution)/shard_map/all_to_all | solution.py:252
  109.3 0.6 fusion
  109.9 0.2 slice_reduce_fusion
  110.1 29.5 %all-to-all-done.2 = bf16[64,8,1024]{2,1,0:T(8,128)(2,1)S(1)} async-done(((bf16[64,8,1024]{2,1,0:T(8,128)(2,1)}), bf16[64,8,1024]{2,1,0:T(8,128)(2,1)S(1)}, u32[]{:S(2)}, u32[]{:S(2)}) %all-to-all-start.2) | async-done | bytes 1048608 | tf_op jit(solution)/shard_map/all_to_all | solution.py:252
  139.6 0.2 convert_reduce_fusion
  139.7 0.7 multiply_convert_fusion
  (25 shorter events, 0.3 us)
Async XLA Ops:
  0.6 55.8 %copy-start.7 = (s32[128]{0:T(128)S(1)}, s32[128]{0:T(128)}, u32[]{:S(2)}) copy-start(s32[128]{0:T(128)} %param.8) | copy-start | bytes 1540
  0.6 58.6 %copy-start.4 = (f32[8192]{0:T(1024)S(1)}, f32[8192]{0:T(1024)}, u32[]{:S(2)}) copy-start(f32[8192]{0:T(1024)} %param.6) | copy-start | bytes 98308
  0.7 58.4 %copy-start.6 = (s32[624]{0:T(1024)S(1)}, s32[624]{0:T(1024)}, u32[]{:S(2)}) copy-start(s32[624]{0:T(1024)} %param.9) | copy-start | bytes 7492
  54.5 4.5 %collective-permute-start = (bf16[64,8,1024]{2,1,0:T(8,128)(2,1)S(1)}, bf16[64,8,1024]{2,1,0:T(8,128)(2,1)S(1)}, u32[]{:S(2)}, u32[]{:S(2)}) collective-permute-start(bf16[64,8,1024]{2,1,0:T(8,128)(2,1)S(1)} %all_to_all.15.got_ref), channel_id=1, source_target_pairs={{0,8},{8,0},{1,9},{9,1},{2,10},{10,2},{3,11},{11,3},{4,12},{12,4},... | collective-permute-start | bytes 3145736 | tf_op jit(solution)/shard_map/ppermute | solution.py:18
  65.4 16.9 %copy-start.2 = (bf16[2,128,624]{2,1,0:T(8,128)(2,1)}, bf16[2,128,624]{2,1,0:T(8,128)(2,1)S(1)}, u32[]{:S(2)}) copy-start(bf16[2,128,624]{2,1,0:T(8,128)(2,1)S(1)} %get-tuple-element.13.lefts_ref) | copy-start | bytes 958468
  65.4 3.1 %collective-permute-start.1 = (f32[4,128]{1,0:T(4,128)S(1)}, f32[4,128]{1,0:T(4,128)S(1)}, u32[]{:S(2)}, u32[]{:S(2)}) collective-permute-start(f32[4,128]{1,0:T(4,128)S(1)} %slice_bitcast_fusion), channel_id=1, source_target_pairs={{0,8},{8,0},{1,9},{9,1},{2,10},{10,2},{3,11},{11,3},{4,12},{12,4},... | collective-permute-start | bytes 6152 | tf_op jit(solution)/shard_map/ppermute | solution.py:18
  69.2 22.7 %all-to-all-start.1 = ((f32[64,4,128]{2,1,0:T(4,128)}), f32[64,4,128]{2,1,0:T(4,128)S(1)}, u32[]{:S(2)}, u32[]{:S(2)}) async-start(f32[64,4,128]{2,1,0:T(4,128)} %pair.1.pair_ref), calls=%async_computation.1 | async-start | bytes 262144 | tf_op jit(solution)/shard_map/all_to_all | solution.py:214
  82.3 10.7 %collective-permute-start.2 = (bf16[2,64,8,1024]{3,2,1,0:T(8,128)(2,1)}, bf16[2,64,8,1024]{3,2,1,0:T(8,128)(2,1)S(1)}, u32[]{:S(2)}, u32[]{:S(2)}) collective-permute-start(bf16[2,64,8,1024]{3,2,1,0:T(8,128)(2,1)} %send.1), channel_id=1, source_target_pairs={{0,8},{8,0},{1,9},{9,1},{2,10},{10,2},{3,11},{11,3},{4,12},{12,4},... | collective-permute-start | bytes 6291464 | tf_op jit(solution)/shard_map/ppermute | solution.py:18
  84.2 1.0 copy-start.3
  90.6 1.3 copy-start
  93.0 1.6 %copy-start.1 = (f32[64,8,1024]{2,1,0:T(8,128)S(1)}, f32[64,8,1024]{2,1,0:T(8,128)}, u32[]{:S(2)}) copy-start(f32[64,8,1024]{2,1,0:T(8,128)} %copy-done) | copy-start | bytes 6291460
  96.4 43.3 %copy-start.5 = (bf16[8,1024]{1,0:T(8,128)(2,1)S(1)}, bf16[8,1024]{1,0:T(8,128)(2,1)}, u32[]{:S(2)}) copy-start(bf16[8,1024]{1,0:T(8,128)(2,1)} %param.5) | copy-start | bytes 49156
  96.4 43.1 %all-to-all-start.2 = ((bf16[64,8,1024]{2,1,0:T(8,128)(2,1)}), bf16[64,8,1024]{2,1,0:T(8,128)(2,1)S(1)}, u32[]{:S(2)}, u32[]{:S(2)}) async-start(bf16[64,8,1024]{2,1,0:T(8,128)(2,1)} %pieces.1), calls=%async_computation.2 | async-start | bytes 2097152 | tf_op jit(solution)/shard_map/all_to_all | solution.py:252

commit v3 on v2

--- a/solution.py
+++ b/solution.py
@@ -36,7 +36,7 @@
 
 
 def logits_kernel(start_ref, got_ref, swapped_ref, gain_ref, head_ref, targets_ref, banned_ref,
-                  lefts_ref, stats_ref, inverse_ref, normed_ref, logits_ref, chunk_ref, semaphores, *, n_z, n_y):
+                  lefts_ref, stats_ref, inverse_ref, chunk_ref, normed_ref, logits_ref, semaphores, *, n_z, n_y):
     k, width = got_ref.shape[1:]
     tokens, full_width = normed_ref.shape
     vocab_rows = head_ref.shape[0]
@@ -83,8 +83,8 @@
     for i, row in enumerate((top, total, dot, target_logit)):
         stats_ref[0, i : i + 1, :] = row
         stats_ref[1, i : i + 1, :] = swap_halves(row)
-    lefts_ref[0] = jnp.where(is_target, 0.0, shifted).T.astype(jnp.bfloat16)
-    lefts_ref[1] = is_target.astype(jnp.float32).T.astype(jnp.bfloat16)
+    lefts_ref[:tokens, :] = jnp.where(is_target, 0.0, shifted).T.astype(jnp.bfloat16)
+    lefts_ref[tokens:, :] = is_target.astype(jnp.float32).T.astype(jnp.bfloat16)
 
 
 def pair_kernel(mine_ref, theirs_ref, out_ref):
@@ -100,36 +100,24 @@
     out_ref[...] = jnp.broadcast_to(pair[None], out_ref.shape)
 
 
-def terms_kernel(mine_ref, pair_ref, lefts_ref, head_ref, terms_ref, picks_ref, chunk_ref, semaphores,
-                 *, n_z, n_y, slot):
-    k, width = picks_ref.shape[-2:]
-    half = lefts_ref.shape[1] // 2
-    for y in range(n_y):
-        head_copy(head_ref, chunk_ref, semaphores, y, width).start()
-    here = slice(slot * half, (slot + 1) * half)
-    share = to_column(jnp.exp(mine_ref[0, 0:1, :] - pair_ref[0, 0:1, :]))[here]
-    lefts = jnp.concatenate([lefts_ref[0, here], lefts_ref[1, here]], axis=0)
+def terms_kernel(mine_ref, pair_ref, lefts_ref, head_ref, send_ref, keep_ref, keep_picks_ref, *, n_z, n_y):
+    k, width = keep_ref.shape[1:]
+    tokens = lefts_ref.shape[0] // 2
+    half = tokens // 2
+    share = to_column(jnp.exp(mine_ref[0, 0:1, :] - pair_ref[0, 0:1, :]))
 
     @pl.loop(0, n_y)
     def _(y):
-        head_copy(head_ref, chunk_ref, semaphores, y, width).wait()
         columns = pl.ds(pl.multiple_of(y * width, width), width)
-        terms = jnp.dot(lefts, chunk_ref[:, columns], preferred_element_type=jnp.float32)
-        scaled = terms[:half] * share
+        terms = jnp.dot(lefts_ref[...], head_ref[:, columns], preferred_element_type=jnp.float32)
+        scaled = terms[:tokens] * share
         for z in range(n_z):
-            rows = slice(z * k, (z + 1) * k)
-            terms_ref[z * n_y + y] = scaled[rows].astype(terms_ref.dtype)
-            picks_ref[z * n_y + y] = terms[half:][rows].astype(picks_ref.dtype)
-
-
-def send_kernel(mine_ref, pair_ref, lefts_ref, head_ref, send_ref, chunk_ref, semaphores, *, n_z, n_y):
-    terms_kernel(mine_ref, pair_ref, lefts_ref, head_ref, send_ref.at[0], send_ref.at[1], chunk_ref, semaphores,
-                 n_z=n_z, n_y=n_y, slot=1)
-
-
-def keep_kernel(mine_ref, pair_ref, lefts_ref, head_ref, keep_ref, keep_picks_ref, chunk_ref, semaphores, *, n_z, n_y):
-    terms_kernel(mine_ref, pair_ref, lefts_ref, head_ref, keep_ref, keep_picks_ref, chunk_ref, semaphores,
-                 n_z=n_z, n_y=n_y, slot=0)
+            own = slice(z * k, (z + 1) * k)
+            other = slice(half + z * k, half + (z + 1) * k)
+            keep_ref[z * n_y + y] = scaled[own]
+            send_ref[0, z * n_y + y] = scaled[other].astype(jnp.bfloat16)
+            keep_picks_ref[z * n_y + y] = terms[tokens:][own].astype(jnp.bfloat16)
+            send_ref[1, z * n_y + y] = terms[tokens:][other].astype(jnp.bfloat16)
 
 
 def combine_kernel(pair_ref, everyone_ref, loss_ref, columns_ref, *, full_width):
@@ -183,7 +171,6 @@
     f32, bf16 = jnp.float32, jnp.bfloat16
     struct = jax.ShapeDtypeStruct
     head = pltpu.with_memory_space_constraint(lm_head, pltpu.HBM)
-    head_scratch = [pltpu.VMEM(lm_head.shape, bf16), pltpu.SemaphoreType.DMA((tensor_count,))]
 
     by_core = targets.reshape(z_count, CORES, own_tokens)
     row_targets = jnp.where(core_index == 0, by_core, by_core[:, ::-1]).transpose(1, 0, 2).reshape(1, tokens)
@@ -195,13 +182,15 @@
     swapped = swap_cores(got)
 
     matmul_flops = 2 * tokens * vocab_rows * full_width
-    lefts, mine, inverse = pl.pallas_call(
+    lefts, mine, inverse, on_chip = pl.pallas_call(
         functools.partial(logits_kernel, n_z=z_count, n_y=tensor_count),
-        out_shape=(struct((2, tokens, vocab_rows), bf16), struct((2, 4, tokens), f32), struct((tokens, 128), f32)),
+        out_shape=(struct((2 * tokens, vocab_rows), bf16), struct((2, 4, tokens), f32), struct((tokens, 128), f32),
+                   struct(lm_head.shape, bf16)),
         in_specs=[SMEM, VMEM, VMEM, VMEM, HBM, VMEM, VMEM],
-        out_specs=(VMEM,) * 3,
-        scratch_shapes=[pltpu.VMEM((tokens, full_width), bf16), pltpu.VMEM((vocab_rows, tokens), f32)] + head_scratch,
-        compiler_params=pltpu.CompilerParams(vmem_limit_bytes=32 * MIB),
+        out_specs=(VMEM,) * 4,
+        scratch_shapes=[pltpu.VMEM((tokens, full_width), bf16), pltpu.VMEM((vocab_rows, tokens), f32),
+                        pltpu.SemaphoreType.DMA((tensor_count,))],
+        compiler_params=pltpu.CompilerParams(vmem_limit_bytes=24 * MIB),
         cost_estimate=pl.CostEstimate(flops=matmul_flops, bytes_accessed=12 * MIB, transcendentals=tokens * vocab_rows),
         name="logits",
     )(vocab_start.reshape(1), got, swapped, gain.reshape(1, full_width), head, row_targets, banned_rows)
@@ -214,22 +203,16 @@
     everyone = lax.all_to_all(pair, PLANE, 0, 0, tiled=True)
 
     piece = (chips, own_tokens, own_width)
-    def half_terms(kernel, out_shape, weight, name):
-        return pl.pallas_call(
-            functools.partial(kernel, n_z=z_count, n_y=tensor_count),
-            out_shape=out_shape,
-            in_specs=[VMEM, VMEM, VMEM, HBM],
-            out_specs=jax.tree.map(lambda _: VMEM, out_shape),
-            scratch_shapes=head_scratch,
-            compiler_params=pltpu.CompilerParams(vmem_limit_bytes=32 * MIB),
-            cost_estimate=pl.CostEstimate(
-                flops=weight * matmul_flops, bytes_accessed=weight * 13 * MIB, transcendentals=0),
-            name=name,
-        )(mine, pair, lefts, head)
-
-    send = half_terms(send_kernel, struct((2,) + piece, bf16), 1, "send")
+    send, keep, keep_picks = pl.pallas_call(
+        functools.partial(terms_kernel, n_z=z_count, n_y=tensor_count),
+        out_shape=(struct((2,) + piece, bf16), struct(piece, f32), struct(piece, bf16)),
+        in_specs=[VMEM] * 4,
+        out_specs=(VMEM,) * 3,
+        compiler_params=pltpu.CompilerParams(vmem_limit_bytes=24 * MIB),
+        cost_estimate=pl.CostEstimate(flops=2 * matmul_flops, bytes_accessed=16 * MIB, transcendentals=0),
+        name="terms",
+    )(mine, pair, lefts, on_chip)
     received = swap_cores(send)
-    keep, keep_picks = half_terms(keep_kernel, (struct(piece, f32), struct(piece, bf16)), 100, "keep")
 
     loss, columns = pl.pallas_call(
         functools.partial(combine_kernel, full_width=full_width),

time: 141 us -> 132 us (0.936)
  blocking collectives: 53 us -> 72.3 us
  starting transfers between devices: 25.1 us -> 10.8 us
  Pallas kernels: 21.8 us -> 13 us
  local copies, waits for them, and re-layouts: 5.88 us -> 2.01 us
  waiting for transfers between devices: 32.8 us -> 31.3 us
    all_to_all x0 -> x1, blocking collectives: none -> 19.3 us  [local(): everyone = lax.all_to_all(pair, PLANE, 0, 0, tiled=True)]
    all_to_all x1, starting transfers between devices: 12.8 us -> 4.78 us  [local(): lax.all_to_all(pieces, PLANE, 0, 0, tiled=True).astype(f32)]
    pallas_call x2 -> x1, Pallas kernels: 12.1 us -> 4.87 us  [local(): pl.pallas_call(functools.partial(terms_kernel, n_z=z_count, n_y=tensor_co...]
    all_to_all x1 -> x0, starting transfers between devices: 6.42 us -> none  [local(): everyone = lax.all_to_all(pair, PLANE, 0, 0, tiled=True)]
    unnamed x16 -> x8, local copies, waits for them, and re-layouts: 3.89 us -> 0.02 us
    all_to_all x1, waiting for transfers between devices: 29.5 us -> 27.9 us  [local(): lax.all_to_all(pieces, PLANE, 0, 0, tiled=True).astype(f32)]
  transfers between devices with their start and end apart: 5 -> 4, of which waited for: 3 -> 3; matrix products, arithmetic and copies ran while one was open for 1% -> 1% of each run, Pallas kernels for 5% -> 0%
where the time goes in v3:
time: 132 us; the launch traced here: 131 us
  blocking collectives  72.3 us (55%)
  waiting for transfers between devices  31.3 us (24%)
  Pallas kernels  13 us (10%)
  starting transfers between devices  10.8 us (8%)
  local copies, waits for them, and re-layouts  2.01 us (2%)
    all_to_all x1, blocking collectives, local(): got = lax.all_to_all(sent, PLANE, 0, 0, tiled=True)  53 us
    all_to_all x1, waiting for transfers between devices, local(): lax.all_to_all(pieces, PLANE, 0, 0, tiled=True).astype(f32)  27.9 us
    all_to_all x1, blocking collectives, local(): everyone = lax.all_to_all(pair, PLANE, 0, 0, tiled=True)  19.3 us
    pallas_call x1, Pallas kernels, local(): pl.pallas_call(functools.partial(logits_kernel, n_z=z_count, n_y=tensor_c...  6.11 us
    ppermute x3, starting transfers between devices, swap_cores(): return lax.ppermute(values, 'core', [(0, 1), (1, 0)])  6.06 us
    pallas_call x1, Pallas kernels, local(): pl.pallas_call(functools.partial(terms_kernel, n_z=z_count, n_y=tensor_co...  4.87 us
    all_to_all x1, starting transfers between devices, local(): lax.all_to_all(pieces, PLANE, 0, 0, tiled=True).astype(f32)  4.78 us
    ppermute x3, waiting for transfers between devices, swap_cores(): return lax.ppermute(values, 'core', [(0, 1), (1, 0)])  3.35 us
  transfers between devices with their start and end apart: 4, of which 3 were waited for; matrix products, arithmetic and copies ran while one was open for 1% of the time, Pallas kernels for 0%

profile of v3, /device:TPU:14, one launch (start us, length us, event | category | flops | bytes accessed | tf_op | source)
XLA Modules:
  0.0 131.2 jit_solution(16226604177742235743)
XLA Ops:
  0.7 0.8 broadcast_in_dim.4
  1.5 53.0 %all_to_all.15.got_ref = bf16[64,8,1024]{2,1,0:T(8,128)(2,1)S(1)} all-to-all(bf16[64,8,1024]{2,1,0:T(8,128)(2,1)S(1)} %broadcast_in_dim.4), channel_id=1, replica_groups=mesh['dp'=8,'z'=8,'core'=2,'tensor'=8] {'z','tensor'}, dimensions={0} | all-to-all | bytes 2097152 | tf_op jit(solution)/shard_map/all_to_all | solution.py:181
  54.5 1.9 %collective-permute-start = (bf16[64,8,1024]{2,1,0:T(8,128)(2,1)S(1)}, bf16[64,8,1024]{2,1,0:T(8,128)(2,1)S(1)}, u32[]{:S(2)}, u32[]{:S(2)}) collective-permute-start(bf16[64,8,1024]{2,1,0:T(8,128)(2,1)S(1)} %all_to_all.15.got_ref), channel_id=1, source_target_pairs={{0,8},{8,0},{1,9},{9,1},{2,10},{10,2},{3,11},{11,3},{4,12},{12,4},... | collective-permute-start | bytes 3145736 | tf_op jit(solution)/shard_map/ppermute | solution.py:18
  56.4 0.0 copy-done.3
  56.5 0.1 reshape.22
  56.6 0.1 reshape.23.targets_ref
  56.7 2.3 %collective-permute-done.swapped_ref = bf16[64,8,1024]{2,1,0:T(8,128)(2,1)S(1)} collective-permute-done((bf16[64,8,1024]{2,1,0:T(8,128)(2,1)S(1)}, bf16[64,8,1024]{2,1,0:T(8,128)(2,1)S(1)}, u32[]{:S(2)}, u32[]{:S(2)}) %collective-permute-start) | collective-permute-done | bytes 1048608 | tf_op jit(solution)/shard_map/ppermute | solution.py:18
  59.1 0.1 broadcast_in_dim.5.banned_ref
  59.2 0.0 copy-done
  59.2 6.1 %logits.1 = (bf16[256,624]{1,0:T(8,128)(2,1)S(1)}, f32[2,4,128]{2,1,0:T(4,128)S(1)}, f32[128,128]{1,0:T(8,128)S(1)}, bf16[624,8192]{1,0:T(8,128)(2,1)S(1)}) custom-call(s32[1]{0:T(128)} %bitcast.start_ref, bf16[64,8,1024]{2,1,0:T(8,128)(2,1)S(1)} %all_to_all.15.got_ref, bf16[64,8,1024]{2,1,0:T(8,128)(2,1)S(1)} %collective-permute-done.swapped_ref, ...), custom_call_target="tpu_custom_call" | custom-call | flops 1308622848 | bytes 12582912 | tf_op jit(solution)/shard_map/logits/pallas_call | solution.py:185
  65.3 2.0 %collective-permute-start.1 = (f32[4,128]{1,0:T(4,128)S(1)}, f32[4,128]{1,0:T(4,128)S(1)}, u32[]{:S(2)}, u32[]{:S(2)}) collective-permute-start(f32[4,128]{1,0:T(4,128)S(1)} %slice_bitcast_fusion), channel_id=1, source_target_pairs={{0,8},{8,0},{1,9},{9,1},{2,10},{10,2},{3,11},{11,3},{4,12},{12,4},... | collective-permute-start | bytes 6152 | tf_op jit(solution)/shard_map/ppermute | solution.py:18
  67.4 1.0 collective-permute-done.1.theirs_ref
  68.4 4.9 %terms.1 = (bf16[2,64,8,1024]{3,2,1,0:T(8,128)(2,1)S(1)}, f32[64,8,1024]{2,1,0:T(8,128)S(1)}, bf16[64,8,1024]{2,1,0:T(8,128)(2,1)S(1)}) custom-call(f32[2,4,128]{2,1,0:T(4,128)S(1)} %get-tuple-element.11.mine_ref, f32[64,4,128]{2,1,0:T(4,128)S(1)} %pair.1.pair_ref, bf16[256,624]{1,0:T(8,128)(2,1)S(1)} %get-tuple-element.15.lefts_ref, ...), custom_call_target="tpu_custom_call" | custom-call | flops 2617245696 | bytes 16777216 | tf_op jit(solution)/shard_map/terms/pallas_call | solution.py:206
  73.3 2.1 %collective-permute-start.2 = (bf16[2,64,8,1024]{3,2,1,0:T(8,128)(2,1)S(1)}, bf16[2,64,8,1024]{3,2,1,0:T(8,128)(2,1)S(1)}, u32[]{:S(2)}, u32[]{:S(2)}) collective-permute-start(bf16[2,64,8,1024]{3,2,1,0:T(8,128)(2,1)S(1)} %get-tuple-element.19), channel_id=1, source_target_pairs={{0,8},{8,0},{1,9},{9,1},{2,10},{10,2},{3,11},{11,3},{4,12},{12,4},... | collective-permute-start | bytes 6291464 | tf_op jit(solution)/shard_map/ppermute | solution.py:18
  75.4 19.3 %all_to_all.16.everyone_ref = f32[64,4,128]{2,1,0:T(4,128)S(1)} all-to-all(f32[64,4,128]{2,1,0:T(4,128)S(1)} %pair.1.pair_ref), channel_id=1, replica_groups=mesh['dp'=8,'z'=8,'core'=2,'tensor'=8] {'z','tensor'}, dimensions={0} | all-to-all | bytes 262144 | tf_op jit(solution)/shard_map/all_to_all | solution.py:203
  94.7 0.2 combine.1
  94.9 0.0 collective-permute-done.2.received_ref
  95.0 1.8 %pieces.1 = bf16[64,8,1024]{2,1,0:T(8,128)(2,1)} custom-call(f32[128,128]{1,0:T(8,128)S(1)} %get-tuple-element.14.columns_ref, f32[64,8,1024]{2,1,0:T(8,128)S(1)} %get-tuple-element.17.keep_ref, bf16[64,8,1024]{2,1,0:T(8,128)(2,1)S(1)} %get-tuple-element.18.keep_picks_ref, bf16[2,64,8,1024]{3,2,1,0:T(8,128)(2,1)S(1)} %collective-permute-done.2.received_ref), custom_call_target="tpu_custom_call" | custom-call | bytes 8388608 | tf_op jit(solution)/shard_map/pieces/pallas_call | solution.py:226
  96.7 4.8 %all-to-all-start.2 = ((bf16[64,8,1024]{2,1,0:T(8,128)(2,1)}), bf16[64,8,1024]{2,1,0:T(8,128)(2,1)S(1)}, u32[]{:S(2)}, u32[]{:S(2)}) async-start(bf16[64,8,1024]{2,1,0:T(8,128)(2,1)} %pieces.1), calls=%async_computation.2 | async-start | bytes 2097152 | tf_op jit(solution)/shard_map/all_to_all | solution.py:235
  101.6 0.6 fusion
  102.2 0.2 slice_reduce_fusion
  102.4 27.9 %all-to-all-done.2 = bf16[64,8,1024]{2,1,0:T(8,128)(2,1)S(1)} async-done(((bf16[64,8,1024]{2,1,0:T(8,128)(2,1)}), bf16[64,8,1024]{2,1,0:T(8,128)(2,1)S(1)}, u32[]{:S(2)}, u32[]{:S(2)}) %all-to-all-start.2) | async-done | bytes 1048608 | tf_op jit(solution)/shard_map/all_to_all | solution.py:235
  130.3 0.2 convert_reduce_fusion
  130.5 0.7 multiply_convert_fusion
  (15 shorter events, 0.1 us)
Async XLA Ops:
  0.6 55.8 %copy-start.3 = (s32[128]{0:T(128)S(1)}, s32[128]{0:T(128)}, u32[]{:S(2)}) copy-start(s32[128]{0:T(128)} %param.8) | copy-start | bytes 1540
  0.6 58.6 %copy-start = (f32[8192]{0:T(1024)S(1)}, f32[8192]{0:T(1024)}, u32[]{:S(2)}) copy-start(f32[8192]{0:T(1024)} %param.6) | copy-start | bytes 98308
  0.7 58.4 %copy-start.2 = (s32[624]{0:T(1024)S(1)}, s32[624]{0:T(1024)}, u32[]{:S(2)}) copy-start(s32[624]{0:T(1024)} %param.9) | copy-start | bytes 7492
  54.5 4.5 %collective-permute-start = (bf16[64,8,1024]{2,1,0:T(8,128)(2,1)S(1)}, bf16[64,8,1024]{2,1,0:T(8,128)(2,1)S(1)}, u32[]{:S(2)}, u32[]{:S(2)}) collective-permute-start(bf16[64,8,1024]{2,1,0:T(8,128)(2,1)S(1)} %all_to_all.15.got_ref), channel_id=1, source_target_pairs={{0,8},{8,0},{1,9},{9,1},{2,10},{10,2},{3,11},{11,3},{4,12},{12,4},... | collective-permute-start | bytes 3145736 | tf_op jit(solution)/shard_map/ppermute | solution.py:18
  65.3 3.1 %collective-permute-start.1 = (f32[4,128]{1,0:T(4,128)S(1)}, f32[4,128]{1,0:T(4,128)S(1)}, u32[]{:S(2)}, u32[]{:S(2)}) collective-permute-start(f32[4,128]{1,0:T(4,128)S(1)} %slice_bitcast_fusion), channel_id=1, source_target_pairs={{0,8},{8,0},{1,9},{9,1},{2,10},{10,2},{3,11},{11,3},{4,12},{12,4},... | collective-permute-start | bytes 6152 | tf_op jit(solution)/shard_map/ppermute | solution.py:18
  73.3 21.6 %collective-permute-start.2 = (bf16[2,64,8,1024]{3,2,1,0:T(8,128)(2,1)S(1)}, bf16[2,64,8,1024]{3,2,1,0:T(8,128)(2,1)S(1)}, u32[]{:S(2)}, u32[]{:S(2)}) collective-permute-start(bf16[2,64,8,1024]{3,2,1,0:T(8,128)(2,1)S(1)} %get-tuple-element.19), channel_id=1, source_target_pairs={{0,8},{8,0},{1,9},{9,1},{2,10},{10,2},{3,11},{11,3},{4,12},{12,4},... | collective-permute-start | bytes 6291464 | tf_op jit(solution)/shard_map/ppermute | solution.py:18
  96.7 33.7 %copy-start.1 = (bf16[8,1024]{1,0:T(8,128)(2,1)S(1)}, bf16[8,1024]{1,0:T(8,128)(2,1)}, u32[]{:S(2)}) copy-start(bf16[8,1024]{1,0:T(8,128)(2,1)} %param.5) | copy-start | bytes 49156
  96.7 33.6 %all-to-all-start.2 = ((bf16[64,8,1024]{2,1,0:T(8,128)(2,1)}), bf16[64,8,1024]{2,1,0:T(8,128)(2,1)S(1)}, u32[]{:S(2)}, u32[]{:S(2)}) async-start(bf16[64,8,1024]{2,1,0:T(8,128)(2,1)} %pieces.1), calls=%async_computation.2 | async-start | bytes 2097152 | tf_op jit(solution)/shard_map/all_to_all | solution.py:235

commit v4 on v3

--- a/solution.py
+++ b/solution.py
@@ -32,7 +32,14 @@
     n = row.shape[1]
     square = jnp.broadcast_to(row, (n, n))
     here = lax.broadcasted_iota(jnp.int32, (n, n), 0) == lax.broadcasted_iota(jnp.int32, (n, n), 1)
-    return jnp.sum(jnp.where(here, square, 0.0), axis=1, keepdims=True)
+    return jnp.sum(jnp.where(here, square, jnp.zeros_like(square)), axis=1, keepdims=True)
+
+
+def to_row(column):
+    n = column.shape[0]
+    square = jnp.broadcast_to(column, (n, n))
+    here = lax.broadcasted_iota(jnp.int32, (n, n), 0) == lax.broadcasted_iota(jnp.int32, (n, n), 1)
+    return jnp.sum(jnp.where(here, square, 0.0), axis=0, keepdims=True)
 
 
 def logits_kernel(start_ref, got_ref, swapped_ref, gain_ref, head_ref, targets_ref, banned_ref,
@@ -67,24 +74,25 @@
         head_copy(head_ref, chunk_ref, semaphores, y, width).wait()
         columns = pl.ds(pl.multiple_of(y * width, width), width)
         logits_ref[...] += lax.dot_general(
-            chunk_ref[:, columns], normed_ref[:, columns], (((1,), (1,)), ((), ())),
+            normed_ref[:, columns], chunk_ref[:, columns], (((1,), (1,)), ((), ())),
             preferred_element_type=jnp.float32)
 
     logits = logits_ref[...]
-    ids = start_ref[0] + lax.broadcasted_iota(jnp.int32, (vocab_rows, tokens), 0)
-    is_target = ids == targets_ref[...]
+    ids = start_ref[0] + lax.broadcasted_iota(jnp.int32, (tokens, vocab_rows), 1)
+    is_target = ids == to_column(targets_ref[...])
     allowed = (banned_ref[...] == 0) | is_target
-    top = jnp.max(jnp.where(allowed, logits, LOWEST), axis=0, keepdims=True)
+    top = jnp.max(jnp.where(allowed, logits, LOWEST), axis=1, keepdims=True)
     below = logits - top
     shifted = jnp.where(allowed, jnp.exp(below), 0.0)
-    total = jnp.sum(shifted, axis=0, keepdims=True)
-    dot = jnp.sum(jnp.where(allowed, shifted * below, 0.0), axis=0, keepdims=True)
-    target_logit = jnp.sum(jnp.where(is_target, logits, 0.0), axis=0, keepdims=True)
-    for i, row in enumerate((top, total, dot, target_logit)):
+    total = jnp.sum(shifted, axis=1, keepdims=True)
+    dot = jnp.sum(jnp.where(allowed, shifted * below, 0.0), axis=1, keepdims=True)
+    target_logit = jnp.sum(jnp.where(is_target, logits, 0.0), axis=1, keepdims=True)
+    for i, column in enumerate((top, total, dot, target_logit)):
+        row = to_row(column)
         stats_ref[0, i : i + 1, :] = row
         stats_ref[1, i : i + 1, :] = swap_halves(row)
-    lefts_ref[:tokens, :] = jnp.where(is_target, 0.0, shifted).T.astype(jnp.bfloat16)
-    lefts_ref[tokens:, :] = is_target.astype(jnp.float32).T.astype(jnp.bfloat16)
+    lefts_ref[:tokens, :] = jnp.where(is_target, 0.0, shifted).astype(jnp.bfloat16)
+    lefts_ref[tokens:, :] = is_target.astype(jnp.float32).astype(jnp.bfloat16)
 
 
 def pair_kernel(mine_ref, theirs_ref, out_ref):
@@ -175,7 +183,7 @@
     by_core = targets.reshape(z_count, CORES, own_tokens)
     row_targets = jnp.where(core_index == 0, by_core, by_core[:, ::-1]).transpose(1, 0, 2).reshape(1, tokens)
     vocab_start = ((z_index * CORES + core_index) * tensor_count + tensor_index) * vocab_rows
-    banned_rows = jnp.broadcast_to(banned[:, None], (vocab_rows, tokens))
+    banned_rows = banned.reshape(1, vocab_rows)
 
     sent = jnp.broadcast_to(hidden[None], (chips, own_tokens, own_width))
     got = lax.all_to_all(sent, PLANE, 0, 0, tiled=True)
@@ -188,7 +196,7 @@
                    struct(lm_head.shape, bf16)),
         in_specs=[SMEM, VMEM, VMEM, VMEM, HBM, VMEM, VMEM],
         out_specs=(VMEM,) * 4,
-        scratch_shapes=[pltpu.VMEM((tokens, full_width), bf16), pltpu.VMEM((vocab_rows, tokens), f32),
+        scratch_shapes=[pltpu.VMEM((tokens, full_width), bf16), pltpu.VMEM((tokens, vocab_rows), f32),
                         pltpu.SemaphoreType.DMA((tensor_count,))],
         compiler_params=pltpu.CompilerParams(vmem_limit_bytes=24 * MIB),
         cost_estimate=pl.CostEstimate(flops=matmul_flops, bytes_accessed=12 * MIB, transcendentals=tokens * vocab_rows),

time: 132 us -> 132 us (level)
  no operation moved by 1% of the time
where the time goes in v4:
time: 132 us; the launch traced here: 131 us
  blocking collectives  72.3 us (55%)
  waiting for transfers between devices  31.3 us (24%)
  Pallas kernels  13.4 us (10%)
  starting transfers between devices  10.8 us (8%)
  local copies, waits for them, and re-layouts  1.88 us (1%)
    all_to_all x1, blocking collectives, local(): got = lax.all_to_all(sent, PLANE, 0, 0, tiled=True)  53 us
    all_to_all x1, waiting for transfers between devices, local(): lax.all_to_all(pieces, PLANE, 0, 0, tiled=True).astype(f32)  28 us
    all_to_all x1, blocking collectives, local(): everyone = lax.all_to_all(pair, PLANE, 0, 0, tiled=True)  19.3 us
    pallas_call x1, Pallas kernels, local(): pl.pallas_call(functools.partial(logits_kernel, n_z=z_count, n_y=tensor_c...  6.65 us
    ppermute x3, starting transfers between devices, swap_cores(): return lax.ppermute(values, 'core', [(0, 1), (1, 0)])  6.03 us
    all_to_all x1, starting transfers between devices, local(): lax.all_to_all(pieces, PLANE, 0, 0, tiled=True).astype(f32)  4.78 us
    pallas_call x1, Pallas kernels, local(): pl.pallas_call(functools.partial(terms_kernel, n_z=z_count, n_y=tensor_co...  4.74 us
    ppermute x3, waiting for transfers between devices, swap_cores(): return lax.ppermute(values, 'core', [(0, 1), (1, 0)])  3.33 us
  transfers between devices with their start and end apart: 4, of which 3 were waited for; matrix products, arithmetic and copies ran while one was open for 1% of the time, Pallas kernels for 0%

profile of v4, /device:TPU:14, one launch (start us, length us, event | category | flops | bytes accessed | tf_op | source)
XLA Modules:
  0.0 131.4 jit_solution(1439860615178906735)
XLA Ops:
  0.6 0.0 copy-start.2
  0.7 0.8 broadcast_in_dim.2
  1.5 53.0 %all_to_all.15.got_ref = bf16[64,8,1024]{2,1,0:T(8,128)(2,1)S(1)} all-to-all(bf16[64,8,1024]{2,1,0:T(8,128)(2,1)S(1)} %broadcast_in_dim.2), channel_id=1, replica_groups=mesh['dp'=8,'z'=8,'core'=2,'tensor'=8] {'z','tensor'}, dimensions={0} | all-to-all | bytes 2097152 | tf_op jit(solution)/shard_map/all_to_all | solution.py:189
  54.5 1.9 %collective-permute-start = (bf16[64,8,1024]{2,1,0:T(8,128)(2,1)S(1)}, bf16[64,8,1024]{2,1,0:T(8,128)(2,1)S(1)}, u32[]{:S(2)}, u32[]{:S(2)}) collective-permute-start(bf16[64,8,1024]{2,1,0:T(8,128)(2,1)S(1)} %all_to_all.15.got_ref), channel_id=1, source_target_pairs={{0,8},{8,0},{1,9},{9,1},{2,10},{10,2},{3,11},{11,3},{4,12},{12,4},... | collective-permute-start | bytes 3145736 | tf_op jit(solution)/shard_map/ppermute | solution.py:18
  56.4 0.0 copy-done.2
  56.5 0.0 copy-done.3
  56.5 0.1 reshape.24
  56.6 0.1 reshape.25.targets_ref
  56.7 2.3 %collective-permute-done.swapped_ref = bf16[64,8,1024]{2,1,0:T(8,128)(2,1)S(1)} collective-permute-done((bf16[64,8,1024]{2,1,0:T(8,128)(2,1)S(1)}, bf16[64,8,1024]{2,1,0:T(8,128)(2,1)S(1)}, u32[]{:S(2)}, u32[]{:S(2)}) %collective-permute-start) | collective-permute-done | bytes 1048608 | tf_op jit(solution)/shard_map/ppermute | solution.py:18
  59.1 6.7 %logits.1 = (bf16[256,624]{1,0:T(8,128)(2,1)S(1)}, f32[2,4,128]{2,1,0:T(4,128)S(1)}, f32[128,128]{1,0:T(8,128)S(1)}, bf16[624,8192]{1,0:T(8,128)(2,1)S(1)}) custom-call(s32[1]{0:T(128)} %bitcast.start_ref, bf16[64,8,1024]{2,1,0:T(8,128)(2,1)S(1)} %all_to_all.15.got_ref, bf16[64,8,1024]{2,1,0:T(8,128)(2,1)S(1)} %collective-permute-done.swapped_ref, ...), custom_call_target="tpu_custom_call" | custom-call | flops 1308622848 | bytes 12582912 | tf_op jit(solution)/shard_map/logits/pallas_call | solution.py:193
  65.7 2.0 %collective-permute-start.1 = (f32[4,128]{1,0:T(4,128)S(1)}, f32[4,128]{1,0:T(4,128)S(1)}, u32[]{:S(2)}, u32[]{:S(2)}) collective-permute-start(f32[4,128]{1,0:T(4,128)S(1)} %slice_bitcast_fusion), channel_id=1, source_target_pairs={{0,8},{8,0},{1,9},{9,1},{2,10},{10,2},{3,11},{11,3},{4,12},{12,4},... | collective-permute-start | bytes 6152 | tf_op jit(solution)/shard_map/ppermute | solution.py:18
  67.8 1.0 collective-permute-done.1.theirs_ref
  68.8 4.7 %terms.1 = (bf16[2,64,8,1024]{3,2,1,0:T(8,128)(2,1)S(1)}, f32[64,8,1024]{2,1,0:T(8,128)S(1)}, bf16[64,8,1024]{2,1,0:T(8,128)(2,1)S(1)}) custom-call(f32[2,4,128]{2,1,0:T(4,128)S(1)} %get-tuple-element.11.mine_ref, f32[64,4,128]{2,1,0:T(4,128)S(1)} %pair.1.pair_ref, bf16[256,624]{1,0:T(8,128)(2,1)S(1)} %get-tuple-element.15.lefts_ref, ...), custom_call_target="tpu_custom_call" | custom-call | flops 2617245696 | bytes 16777216 | tf_op jit(solution)/shard_map/terms/pallas_call | solution.py:214
  73.6 2.1 %collective-permute-start.2 = (bf16[2,64,8,1024]{3,2,1,0:T(8,128)(2,1)S(1)}, bf16[2,64,8,1024]{3,2,1,0:T(8,128)(2,1)S(1)}, u32[]{:S(2)}, u32[]{:S(2)}) collective-permute-start(bf16[2,64,8,1024]{3,2,1,0:T(8,128)(2,1)S(1)} %get-tuple-element.19), channel_id=1, source_target_pairs={{0,8},{8,0},{1,9},{9,1},{2,10},{10,2},{3,11},{11,3},{4,12},{12,4},... | collective-permute-start | bytes 6291464 | tf_op jit(solution)/shard_map/ppermute | solution.py:18
  75.7 19.3 %all_to_all.16.everyone_ref = f32[64,4,128]{2,1,0:T(4,128)S(1)} all-to-all(f32[64,4,128]{2,1,0:T(4,128)S(1)} %pair.1.pair_ref), channel_id=1, replica_groups=mesh['dp'=8,'z'=8,'core'=2,'tensor'=8] {'z','tensor'}, dimensions={0} | all-to-all | bytes 262144 | tf_op jit(solution)/shard_map/all_to_all | solution.py:211
  95.0 0.2 combine.1
  95.2 0.0 collective-permute-done.2.received_ref
  95.2 1.8 %pieces.1 = bf16[64,8,1024]{2,1,0:T(8,128)(2,1)} custom-call(f32[128,128]{1,0:T(8,128)S(1)} %get-tuple-element.14.columns_ref, f32[64,8,1024]{2,1,0:T(8,128)S(1)} %get-tuple-element.17.keep_ref, bf16[64,8,1024]{2,1,0:T(8,128)(2,1)S(1)} %get-tuple-element.18.keep_picks_ref, bf16[2,64,8,1024]{3,2,1,0:T(8,128)(2,1)S(1)} %collective-permute-done.2.received_ref), custom_call_target="tpu_custom_call" | custom-call | bytes 8388608 | tf_op jit(solution)/shard_map/pieces/pallas_call | solution.py:234
  97.0 4.8 %all-to-all-start.2 = ((bf16[64,8,1024]{2,1,0:T(8,128)(2,1)}), bf16[64,8,1024]{2,1,0:T(8,128)(2,1)S(1)}, u32[]{:S(2)}, u32[]{:S(2)}) async-start(bf16[64,8,1024]{2,1,0:T(8,128)(2,1)} %pieces.1), calls=%async_computation.2 | async-start | bytes 2097152 | tf_op jit(solution)/shard_map/all_to_all | solution.py:243
  101.8 0.6 fusion
  102.4 0.2 slice_reduce_fusion
  102.6 28.0 %all-to-all-done.2 = bf16[64,8,1024]{2,1,0:T(8,128)(2,1)S(1)} async-done(((bf16[64,8,1024]{2,1,0:T(8,128)(2,1)}), bf16[64,8,1024]{2,1,0:T(8,128)(2,1)S(1)}, u32[]{:S(2)}, u32[]{:S(2)}) %all-to-all-start.2) | async-done | bytes 1048608 | tf_op jit(solution)/shard_map/all_to_all | solution.py:243
  130.6 0.2 convert_reduce_fusion
  130.8 0.7 multiply_convert_fusion
  (15 shorter events, 0.1 us)
Async XLA Ops:
  0.6 55.8 %copy-start.2 = (s32[624]{0:T(1024)S(1)}, s32[624]{0:T(1024)}, u32[]{:S(2)}) copy-start(s32[624]{0:T(1024)} %param.9) | copy-start | bytes 7492
  0.6 55.8 %copy-start.3 = (s32[128]{0:T(128)S(1)}, s32[128]{0:T(128)}, u32[]{:S(2)}) copy-start(s32[128]{0:T(128)} %param.8) | copy-start | bytes 1540
  0.7 58.4 %copy-start = (f32[8192]{0:T(1024)S(1)}, f32[8192]{0:T(1024)}, u32[]{:S(2)}) copy-start(f32[8192]{0:T(1024)} %param.6) | copy-start | bytes 98308
  54.5 4.5 %collective-permute-start = (bf16[64,8,1024]{2,1,0:T(8,128)(2,1)S(1)}, bf16[64,8,1024]{2,1,0:T(8,128)(2,1)S(1)}, u32[]{:S(2)}, u32[]{:S(2)}) collective-permute-start(bf16[64,8,1024]{2,1,0:T(8,128)(2,1)S(1)} %all_to_all.15.got_ref), channel_id=1, source_target_pairs={{0,8},{8,0},{1,9},{9,1},{2,10},{10,2},{3,11},{11,3},{4,12},{12,4},... | collective-permute-start | bytes 3145736 | tf_op jit(solution)/shard_map/ppermute | solution.py:18
  65.7 3.1 %collective-permute-start.1 = (f32[4,128]{1,0:T(4,128)S(1)}, f32[4,128]{1,0:T(4,128)S(1)}, u32[]{:S(2)}, u32[]{:S(2)}) collective-permute-start(f32[4,128]{1,0:T(4,128)S(1)} %slice_bitcast_fusion), channel_id=1, source_target_pairs={{0,8},{8,0},{1,9},{9,1},{2,10},{10,2},{3,11},{11,3},{4,12},{12,4},... | collective-permute-start | bytes 6152 | tf_op jit(solution)/shard_map/ppermute | solution.py:18
  73.6 21.6 %collective-permute-start.2 = (bf16[2,64,8,1024]{3,2,1,0:T(8,128)(2,1)S(1)}, bf16[2,64,8,1024]{3,2,1,0:T(8,128)(2,1)S(1)}, u32[]{:S(2)}, u32[]{:S(2)}) collective-permute-start(bf16[2,64,8,1024]{3,2,1,0:T(8,128)(2,1)S(1)} %get-tuple-element.19), channel_id=1, source_target_pairs={{0,8},{8,0},{1,9},{9,1},{2,10},{10,2},{3,11},{11,3},{4,12},{12,4},... | collective-permute-start | bytes 6291464 | tf_op jit(solution)/shard_map/ppermute | solution.py:18
  97.0 33.8 %copy-start.1 = (bf16[8,1024]{1,0:T(8,128)(2,1)S(1)}, bf16[8,1024]{1,0:T(8,128)(2,1)}, u32[]{:S(2)}) copy-start(bf16[8,1024]{1,0:T(8,128)(2,1)} %param.5) | copy-start | bytes 49156
  97.0 33.6 %all-to-all-start.2 = ((bf16[64,8,1024]{2,1,0:T(8,128)(2,1)}), bf16[64,8,1024]{2,1,0:T(8,128)(2,1)S(1)}, u32[]{:S(2)}, u32[]{:S(2)}) async-start(bf16[64,8,1024]{2,1,0:T(8,128)(2,1)} %pieces.1), calls=%async_computation.2 | async-start | bytes 2097152 | tf_op jit(solution)/shard_map/all_to_all | solution.py:243
